TPU v7x, 768 devices: a whole 4x8x12 slice. The times are simulated.
768 devices in a mesh: gx: 16 (over y_lo, x, core), gy: 48 (over y_hi, z).
Axes of the slice: x: 4, y: 8 (y_hi: 4, y_lo: 2; y = y_hi * 2 + y_lo), z: 12, core: 2. Of those that a mesh axis runs over, the one named last changes fastest.
Arguments:
- positions: float32 [16, 48, 3, 32], P('gx', 'gy'), may hold values from 0 to 12, as said below
- features: float32 [16, 48, 32, 128], P('gx', 'gy'), may hold values from -6 to 6
- cotangent: float32 [16, 48, 32, 1152], P('gx', 'gy'), may hold values from -6 to 6
- nbr_src: int32 [16, 48, 5, 5, 32], P('gx', 'gy'), may hold values from 0 to 31
- nbr_tgt: int32 [16, 48, 5, 5, 32], P('gx', 'gy'), may hold values from 0 to 31
- pair_mask: int32 [16, 48, 5, 5, 32], P('gx', 'gy'), may hold values 0 or 1
- pair_species: int32 [16, 48, 5, 5, 32], P('gx', 'gy'), may hold values from 0 to 9
- w_in: float32 [8, 32], replicated, may hold values from -2 to 2
- species_emb: float32 [10, 32], replicated, may hold values from -6 to 6
- w_out: float32 [32, 384], replicated, may hold values from -1 to 1
Outputs:
- pos_grad: float32 [16, 48, 3, 32], P('gx', 'gy')
- feat_grad: float32 [16, 48, 32, 128], P('gx', 'gy')
Inputs may be any that keep to these rules, and one draw needn't show every extreme that they name: `positions`: the first two coordinates lie in 0 to 5, the third in 0 to 12.
All inputs are finite; a program needn't handle non-finite values. No bound on the sum of `pair_mask` on one device may be relied on, other than what follows from the above.
Results may differ from a plain program's by a relative error of at most 0.0003.
Values sent between devices are 32-bit elements; how exact they have to be, the bound alone decides.
A program may use at most 32 MiB of HBM per device.

v0:
```python
import math

import jax
import jax.numpy as jnp
from jax import lax
from jax.sharding import PartitionSpec as P

domain_side = 5.0
cutoff = 12.0
soften = 0.25
highest = lax.Precision.HIGHEST


def shifted(value, axis, by):
    peers = lax.axis_size(axis)
    return lax.ppermute(value, axis, [(i, (i + by) % peers) for i in range(peers)])


def harmonics(unit):
    unit_x, unit_y, unit_z = (unit[0], unit[1], unit[2])
    root_three = math.sqrt(3.0)
    root_five = math.sqrt(5.0)
    root_fifteen = math.sqrt(15.0)
    return jnp.stack(
        [
            jnp.ones_like(unit_x),
            root_three * unit_x,
            root_three * unit_y,
            root_three * unit_z,
            root_fifteen * unit_x * unit_y,
            root_fifteen * unit_y * unit_z,
            0.5 * root_five * (2.0 * unit_z * unit_z - unit_x * unit_x - unit_y * unit_y),
            root_fifteen * unit_x * unit_z,
            0.5 * root_fifteen * (unit_x * unit_x - unit_y * unit_y),
        ],
        axis=0,
    )


def tile_geometry(
    tgt_pos,
    src_pos,
    offset,
    src_onehot,
    tgt_onehot,
    live_pair,
    species,
    w_in,
    species_emb,
    w_out,
    channels,
):
    pair_count = src_onehot.shape[0]
    relative = (
        jnp.dot(src_pos, src_onehot.T, precision=highest)
        + offset[:, None]
        - jnp.dot(tgt_pos, tgt_onehot.T, precision=highest)
    )
    distance = jnp.sqrt(jnp.sum(relative * relative, axis=0) + soften)
    scaled = distance / cutoff
    envelope = jnp.where(scaled < 1.0, (1.0 - scaled * scaled) ** 2, 0.0) * live_pair.astype(
        jnp.float32
    )
    orders = jnp.arange(1, w_in.shape[0] + 1, dtype=jnp.int32).astype(jnp.float32)
    radial_basis = (
        math.sqrt(2.0 / cutoff)
        * jnp.sin(orders[None, :] * math.pi * scaled[:, None])
        / distance[:, None]
    )
    picked = (
        species[:, None] == jnp.arange(species_emb.shape[0], dtype=jnp.int32)[None, :]
    ).astype(jnp.float32)
    hidden = jax.nn.silu(
        jnp.dot(radial_basis, w_in, precision=highest)
        + jnp.dot(picked, species_emb, precision=highest)
    )
    radial = (
        jnp.dot(hidden, w_out, precision=highest).reshape(pair_count, 3, channels)
        * envelope[:, None, None]
    )
    shapes = harmonics(relative / distance[None, :])
    return (radial, shapes)


def tile_grads(
    tgt_pos,
    src_pos,
    src_feats,
    offset,
    source_index,
    target_index,
    live_pair,
    species,
    w_in,
    species_emb,
    w_out,
    cot_block,
):
    atom_count = src_feats.shape[0]
    channels = src_feats.shape[1]
    pair_count = source_index.shape[0]
    atom_ids = jnp.arange(atom_count, dtype=jnp.int32)
    src_onehot = (source_index[:, None] == atom_ids[None, :]).astype(jnp.float32)
    tgt_onehot = (target_index[:, None] == atom_ids[None, :]).astype(jnp.float32)

    def geometry(target_xyz, source_xyz):
        return tile_geometry(
            target_xyz,
            source_xyz,
            offset,
            src_onehot,
            tgt_onehot,
            live_pair,
            species,
            w_in,
            species_emb,
            w_out,
            channels,
        )

    (radial, shapes), pullback = jax.vjp(geometry, tgt_pos, src_pos)
    sph = shapes.T
    gathered_feats = jnp.dot(src_onehot, src_feats, precision=highest)
    gathered_cot = jnp.dot(tgt_onehot, cot_block, precision=highest).reshape(
        pair_count, 9, channels
    )
    weighted = gathered_cot * gathered_feats[:, None, :]
    sum_zero = weighted[:, 0] * sph[:, 0:1]
    sum_one = jnp.sum(weighted[:, 1:4] * sph[:, 1:4, None], axis=1)
    sum_two = jnp.sum(weighted[:, 4:9] * sph[:, 4:9, None], axis=1)
    d_radial = jnp.stack([sum_zero, sum_one, sum_two], axis=1)
    d_zero = jnp.sum(radial[:, 0] * weighted[:, 0], axis=1)[:, None]
    d_one = jnp.sum(radial[:, 1][:, None, :] * weighted[:, 1:4], axis=2)
    d_two = jnp.sum(radial[:, 2][:, None, :] * weighted[:, 4:9], axis=2)
    d_shapes = jnp.concatenate([d_zero, d_one, d_two], axis=1).T
    cot_zero = gathered_cot[:, 0] * sph[:, 0:1]
    cot_one = jnp.sum(gathered_cot[:, 1:4] * sph[:, 1:4, None], axis=1)
    cot_two = jnp.sum(gathered_cot[:, 4:9] * sph[:, 4:9, None], axis=1)
    per_pair = radial[:, 0] * cot_zero + radial[:, 1] * cot_one + radial[:, 2] * cot_two
    feat_part = jnp.dot(src_onehot.T, per_pair, precision=highest)
    tgt_part, src_part = pullback((d_radial, d_shapes))
    return (tgt_part, src_part, feat_part)


def fetch_sources(own_block, fetch_plan):
    fetched = {0: own_block}
    for step_to, shift_by, anchor in fetch_plan:
        held = fetched[anchor]
        fetched[step_to] = shifted((held[0], held[1]), "gx", shift_by)
    return fetched


def fetch_targets(own_block, fetch_plan):
    fetched = {0: own_block}
    for step_to, shift_by, anchor in fetch_plan:
        held = fetched[anchor]
        fetched[step_to] = shifted((held[0], held[1]), "gy", shift_by)
    return fetched


def return_sources(partials, return_plan):
    summed_all = partials[0]
    running = partials[0]
    for step_from, shift_by, chained, finish in return_plan:
        outgoing = partials[step_from]
        running = shifted((outgoing[0], outgoing[1]), "gx", shift_by)
        summed_all = jax.tree.map(jnp.add, summed_all, running)
    return summed_all


def return_targets(partials, return_plan):
    summed_all = partials[0]
    running = partials[0]
    for step_from, shift_by, chained, finish in return_plan:
        outgoing = partials[step_from]
        running = shifted(outgoing, "gy", shift_by)
        summed_all = summed_all + running
    return summed_all


def local(
    positions,
    features,
    cotangent,
    nbr_src,
    nbr_tgt,
    pair_mask,
    pair_species,
    w_in,
    species_emb,
    w_out,
):
    own_pos = positions[0, 0]
    own_feats = features[0, 0]
    own_cot = cotangent[0, 0]
    fetch_plan = [(1, -1, 0), (2, -2, 0), (-1, 1, 0), (-2, 2, 0)]
    return_plan = [
        (1, 1, False, True),
        (2, 2, False, True),
        (-1, -1, False, True),
        (-2, -2, False, True),
    ]
    sources = fetch_sources((own_pos, own_feats), fetch_plan)
    targets = fetch_targets((own_pos, own_cot), fetch_plan)
    steps_order = [-2, -1, 0, 1, 2]
    src_pos_stack = jnp.stack([sources[step][0] for step in steps_order])
    src_feat_stack = jnp.stack([sources[step][1] for step in steps_order])
    tgt_pos_stack = jnp.stack([targets[step][0] for step in steps_order])
    cot_stack = jnp.stack([targets[step][1] for step in steps_order])
    rel_steps = (jnp.arange(5, dtype=jnp.int32) - 2).astype(jnp.float32)
    offset_x = jnp.broadcast_to(rel_steps[:, None] * domain_side, (5, 5))
    offset_y = jnp.broadcast_to(-rel_steps[None, :] * domain_side, (5, 5))
    offsets = jnp.stack([offset_x, offset_y, jnp.zeros((5, 5), jnp.float32)], axis=2)
    inner = jax.vmap(tile_grads, in_axes=(0, None, None, 0, 0, 0, 0, 0, None, None, None, 0))
    outer = jax.vmap(inner, in_axes=(None, 0, 0, 0, 0, 0, 0, 0, None, None, None, None))
    tgt_part, src_part, feat_part = outer(
        tgt_pos_stack,
        src_pos_stack,
        src_feat_stack,
        offsets,
        nbr_src[0, 0],
        nbr_tgt[0, 0],
        pair_mask[0, 0],
        pair_species[0, 0],
        w_in,
        species_emb,
        w_out,
        cot_stack,
    )
    tgt_sums = jnp.sum(tgt_part, axis=0)
    src_sums = jnp.sum(src_part, axis=1)
    feat_sums = jnp.sum(feat_part, axis=1)
    src_partials = {}
    tgt_partials = {}
    for step in steps_order:
        tgt_partials[step] = tgt_sums[step + 2]
        src_partials[step] = (src_sums[step + 2], feat_sums[step + 2])
    src_home = return_sources(src_partials, return_plan)
    tgt_home = return_targets(tgt_partials, return_plan)
    pos_total = src_home[0] + tgt_home
    return (pos_total[None, None], src_home[1][None, None])


def solution(mesh):
    in_specs = (
        P("gx", "gy", None, None),
        P("gx", "gy", None, None),
        P("gx", "gy", None, None),
        P("gx", "gy", None, None, None),
        P("gx", "gy", None, None, None),
        P("gx", "gy", None, None, None),
        P("gx", "gy", None, None, None),
        P(),
        P(),
        P(),
    )
    out_specs = (P("gx", "gy", None, None), P("gx", "gy", None, None))
    return jax.shard_map(local, mesh=mesh, in_specs=in_specs, out_specs=out_specs, check_vma=False)
```

profile of v0, /device:TPU:8, one launch (start us, length us, event | category | flops | bytes accessed | tf_op | source)
XLA Modules:
  0.0 163.8 jit_solution(1740716540412908712)
XLA Ops:
  0.6 0.7 copy.118
  1.3 6.1 %collective-permute-start.4 = (f32[3,32]{1,0:T(4,128)S(1)}, f32[3,32]{1,0:T(4,128)S(1)}, u32[]{:S(2)}, u32[]{:S(2)}) collective-permute-start(f32[3,32]{1,0:T(4,128)S(1)} %bitcast.270), channel_id=1, source_target_pairs={{0,2},{1,3},{2,4},{3,5},{4,6},{5,7},{6,8},{7,9},{8,10},{9,11},{10,... | collective-permute-start | bytes 1160 | tf_op jit(solution)/shard_map/ppermute | solution.py:16
  7.4 4.3 %collective-permute-start.5 = (f32[3,32]{1,0:T(4,128)S(1)}, f32[3,32]{1,0:T(4,128)S(1)}, u32[]{:S(2)}, u32[]{:S(2)}) collective-permute-start(f32[3,32]{1,0:T(4,128)S(1)} %bitcast.271), channel_id=1, source_target_pairs={{0,1},{1,2},{2,3},{3,4},{4,5},{5,6},{6,7},{7,8},{8,9},{9,10},{10,1... | collective-permute-start | bytes 1160 | tf_op jit(solution)/shard_map/ppermute | solution.py:16
  11.7 3.4 %collective-permute-start = (f32[3,32]{1,0:T(4,128)S(1)}, f32[3,32]{1,0:T(4,128)S(1)}, u32[]{:S(2)}, u32[]{:S(2)}) collective-permute-start(f32[3,32]{1,0:T(4,128)S(1)} %bitcast.272), channel_id=1, source_target_pairs={{0,96},{48,144},{96,192},{144,240},{192,288},{240,336},{288,384},{... | collective-permute-start | bytes 1160 | tf_op jit(solution)/shard_map/ppermute | solution.py:16
  15.1 1.9 %collective-permute-start.1 = (f32[3,32]{1,0:T(4,128)S(1)}, f32[3,32]{1,0:T(4,128)S(1)}, u32[]{:S(2)}, u32[]{:S(2)}) collective-permute-start(f32[3,32]{1,0:T(4,128)S(1)} %bitcast.273), channel_id=1, source_target_pairs={{0,48},{48,96},{96,144},{144,192},{192,240},{240,288},{288,336},{3... | collective-permute-start | bytes 1160 | tf_op jit(solution)/shard_map/ppermute | solution.py:16
  17.0 5.8 %collective-permute-start.2 = (f32[3,32]{1,0:T(4,128)S(1)}, f32[3,32]{1,0:T(4,128)S(1)}, u32[]{:S(2)}, u32[]{:S(2)}) collective-permute-start(f32[3,32]{1,0:T(4,128)S(1)} %bitcast.274), channel_id=1, source_target_pairs={{0,720},{48,0},{96,48},{144,96},{192,144},{240,192},{288,240},{336... | collective-permute-start | bytes 1160 | tf_op jit(solution)/shard_map/ppermute | solution.py:16
  22.8 0.7 copy.115
  23.6 1.2 fusion.35
  25.1 0.7 copy.117
  25.8 0.7 copy.116
  26.5 0.7 convert_element_type.37
  27.3 2.4 %collective-permute-start.3 = (f32[3,32]{1,0:T(4,128)S(1)}, f32[3,32]{1,0:T(4,128)S(1)}, u32[]{:S(2)}, u32[]{:S(2)}) collective-permute-start(f32[3,32]{1,0:T(4,128)S(1)} %bitcast.275), channel_id=1, source_target_pairs={{0,672},{48,720},{96,0},{144,48},{192,96},{240,144},{288,192},{336... | collective-permute-start | bytes 1160 | tf_op jit(solution)/shard_map/ppermute | solution.py:16
  29.8 10.8 %collective-permute-start.6 = (f32[3,32]{1,0:T(4,128)S(1)}, f32[3,32]{1,0:T(4,128)S(1)}, u32[]{:S(2)}, u32[]{:S(2)}) collective-permute-start(f32[3,32]{1,0:T(4,128)S(1)} %bitcast.276), channel_id=1, source_target_pairs={{0,47},{1,0},{2,1},{3,2},{4,3},{5,4},{6,5},{7,6},{8,7},{9,8},{10,9... | collective-permute-start | bytes 1160 | tf_op jit(solution)/shard_map/ppermute | solution.py:16
  40.6 4.8 %collective-permute-start.7 = (f32[3,32]{1,0:T(4,128)S(1)}, f32[3,32]{1,0:T(4,128)S(1)}, u32[]{:S(2)}, u32[]{:S(2)}) collective-permute-start(f32[3,32]{1,0:T(4,128)S(1)} %bitcast.277), channel_id=1, source_target_pairs={{0,46},{1,47},{2,0},{3,1},{4,2},{5,3},{6,4},{7,5},{8,6},{9,7},{10,... | collective-permute-start | bytes 1160 | tf_op jit(solution)/shard_map/ppermute | solution.py:16
  45.5 3.4 %collective-permute-start.12 = (f32[32,128]{1,0:T(8,128)}, f32[32,128]{1,0:T(8,128)}, u32[]{:S(2)}, u32[]{:S(2)}) collective-permute-start(f32[32,128]{1,0:T(8,128)} %bitcast.265), channel_id=1, source_target_pairs={{0,96},{48,144},{96,192},{144,240},{192,288},{240,336},{288,384},{... | collective-permute-start | bytes 49160 | tf_op jit(solution)/shard_map/ppermute | solution.py:16
  48.9 0.7 constant_dynamic-update-slice_fusion.7
  49.6 1.9 %collective-permute-start.13 = (f32[32,128]{1,0:T(8,128)}, f32[32,128]{1,0:T(8,128)}, u32[]{:S(2)}, u32[]{:S(2)}) collective-permute-start(f32[32,128]{1,0:T(8,128)} %bitcast.266), channel_id=1, source_target_pairs={{0,48},{48,96},{96,144},{144,192},{192,240},{240,288},{288,336},{3... | collective-permute-start | bytes 49160 | tf_op jit(solution)/shard_map/ppermute | solution.py:16
  51.5 5.8 %collective-permute-start.14 = (f32[32,128]{1,0:T(8,128)}, f32[32,128]{1,0:T(8,128)}, u32[]{:S(2)}, u32[]{:S(2)}) collective-permute-start(f32[32,128]{1,0:T(8,128)} %bitcast.267), channel_id=1, source_target_pairs={{0,720},{48,0},{96,48},{144,96},{192,144},{240,192},{288,240},{336... | collective-permute-start | bytes 49160 | tf_op jit(solution)/shard_map/ppermute | solution.py:16
  57.6 2.4 %collective-permute-start.15 = (f32[32,128]{1,0:T(8,128)}, f32[32,128]{1,0:T(8,128)}, u32[]{:S(2)}, u32[]{:S(2)}) collective-permute-start(f32[32,128]{1,0:T(8,128)} %bitcast.268), channel_id=1, source_target_pairs={{0,672},{48,720},{96,0},{144,48},{192,96},{240,144},{288,192},{336... | collective-permute-start | bytes 49160 | tf_op jit(solution)/shard_map/ppermute | solution.py:16
  60.1 1.9 %collective-permute-start.8 = (f32[32,1152]{1,0:T(8,128)}, f32[32,1152]{1,0:T(8,128)}, u32[]{:S(2)}, u32[]{:S(2)}) collective-permute-start(f32[32,1152]{1,0:T(8,128)} %bitcast.257), channel_id=1, source_target_pairs={{0,2},{1,3},{2,4},{3,5},{4,6},{5,7},{6,8},{7,9},{8,10},{9,11},{10,... | collective-permute-start | bytes 442376 | tf_op jit(solution)/shard_map/ppermute | solution.py:16
  62.3 0.6 multiply_divide_fusion
  63.0 1.9 %convolution_add_fusion = f32[5,5,32,32]{3,2,1,0:T(8,128)S(1)} fusion(f32[5,5,32,32]{3,2,1,0:T(8,128)S(1)} %fusion.35, f32[5,5,32]{2,1,0:T(8,128)S(1)} %get-tuple-element.38, f32[5,5,32]{2,1,0:T(8,128)S(1)} %get-tuple-element.36, f32[8]{0:T(128)S(1)} %convert_multiply_fusion, f32[8,32]{1,0:T(8,128)} %param.17), kind=kOutput, calls=%fused_computation.15 | convolution fusion | flops 2502400 | bytes 212256 | tf_op jit(solution)/shard_map/vmap(vmap(jvp()))/dot_general | solution.py:74
  64.9 1.2 fusion.24
  66.1 0.5 reshape.99
  66.7 1.1 broadcast_multiply_fusion.1
  67.7 1.3 fusion.96
  69.4 0.6 copy.58
  70.0 0.6 copy.114
  70.6 2.5 %collective-permute-start.9 = (f32[32,1152]{1,0:T(8,128)}, f32[32,1152]{1,0:T(8,128)S(1)}, u32[]{:S(2)}, u32[]{:S(2)}) collective-permute-start(f32[32,1152]{1,0:T(8,128)} %bitcast.258), channel_id=1, source_target_pairs={{0,1},{1,2},{2,3},{3,4},{4,5},{5,6},{6,7},{7,8},{8,9},{9,10},{10,1... | collective-permute-start | bytes 442376 | tf_op jit(solution)/shard_map/ppermute | solution.py:16
  73.1 0.7 constant_dynamic-update-slice_fusion.14
  73.8 7.6 %collective-permute-start.10 = (f32[32,1152]{1,0:T(8,128)}, f32[32,1152]{1,0:T(8,128)S(1)}, u32[]{:S(2)}, u32[]{:S(2)}) collective-permute-start(f32[32,1152]{1,0:T(8,128)} %bitcast.259), channel_id=1, source_target_pairs={{0,47},{1,0},{2,1},{3,2},{4,3},{5,4},{6,5},{7,6},{8,7},{9,8},{10,9... | collective-permute-start | bytes 442376 | tf_op jit(solution)/shard_map/ppermute | solution.py:16
  81.4 0.7 constant_dynamic-update-slice_fusion.13
  82.2 5.0 %collective-permute-start.11 = (f32[32,1152]{1,0:T(8,128)}, f32[32,1152]{1,0:T(8,128)S(1)}, u32[]{:S(2)}, u32[]{:S(2)}) collective-permute-start(f32[32,1152]{1,0:T(8,128)} %bitcast.260), channel_id=1, source_target_pairs={{0,46},{1,47},{2,0},{3,1},{4,2},{5,3},{6,4},{7,5},{8,6},{9,7},{10,... | collective-permute-start | bytes 442376 | tf_op jit(solution)/shard_map/ppermute | solution.py:16
  87.2 0.7 constant_dynamic-update-slice_fusion.11
  87.9 0.7 constant_dynamic-update-slice_fusion.10
  88.6 1.2 fusion.23
  89.9 0.9 bitcast_dynamic-update-slice_fusion.4
  90.8 0.9 bitcast_dynamic-update-slice_fusion.2
  91.8 0.6 collective-permute-done.11
  92.4 4.2 %convolution_bitcast_fusion = f32[5,5,32,1152]{3,2,0,1:T(8,128)} fusion(f32[5,32,1152]{2,1,0:T(8,128)S(1)} %bitcast_dynamic-update-slice_fusion, s32[5,5,32]{2,1,0:T(8,128)} %bitcast.262), kind=kOutput, calls=%fused_computation | convolution fusion | flops 353920000 | bytes 4426880 | tf_op jit(solution)/shard_map/vmap(vmap())/dot_general | solution.py:124
  96.7 5.8 %reshape.111 = f32[5,5,32,9,128]{4,3,2,0,1:T(8,128)} reshape(f32[5,5,32,1152]{3,2,0,1:T(8,128)} %convolution_bitcast_fusion) | data formatting | bytes 7372800 | tf_op jit(solution)/shard_map/vmap(vmap())/reshape | solution.py:124
  102.5 4.1 %broadcast_multiply_fusion = (f32[5,5,32,9,128]{4,2,1,0,3:T(8,128)S(1)}, f32[5,5,32,9,128]{4,2,1,0,3:T(8,128)S(1)}) fusion(f32[5,5,32,128]{3,2,1,0:T(8,128)S(1)} %fusion.23, f32[5,5,32,9,128]{4,3,2,0,1:T(8,128)} %reshape.111), kind=kLoop, calls=%fused_computation.5 | loop fusion | flops 921600 | bytes 11468800 | tf_op jit(solution)/shard_map/vmap(vmap())/mul | solution.py:127
  106.6 1.2 multiply_reduce_fusion
  107.9 0.7 multiply_reduce_fusion.2
  109.5 1.2 fusion.1
  111.5 1.8 %fusion.40 = (f32[5,5,32]{2,1,0:T(8,128)S(1)}, f32[5,5,32]{2,1,0:T(8,128)S(1)}) fusion(f32[5,5,32]{2,1,0:T(8,128)S(1)} %copy-done.15, f32[5,5,32]{2,1,0:T(8,128)S(1)} %copy-done.12, f32[8]{0:T(128)S(1)} %copy-done.19, f32[5,5,32]{2,1,0:T(8,128)S(1)} %get-tuple-element.38, f32[8,32]{1,0:T(8,128)S(1)} %copy-done.17, ...), kind=kOutput, calls=%fused_computation.73 | convolution fusion | flops 2750400 | bytes 221856 | tf_op jit(solution)/shard_map/vmap(vmap(transpose(jvp())))/dot_general | solution.py:74
  113.6 0.5 convolution_bitcast_fusion.4
  114.4 9.8 %collective-permute-start.23 = (f32[3,32]{1,0:T(4,128)S(1)}, f32[3,32]{1,0:T(4,128)S(1)}, u32[]{:S(2)}, u32[]{:S(2)}) collective-permute-start(f32[3,32]{1,0:T(4,128)S(1)} %get-tuple-element.44), channel_id=1, source_target_pairs={{0,46},{1,47},{2,0},{3,1},{4,2},{5,3},{6,4},{7,5},{8,6},{9,7},{10,... | collective-permute-start | bytes 1160 | tf_op jit(solution)/shard_map/ppermute | solution.py:16
  124.2 3.3 %collective-permute-start.22 = (f32[3,32]{1,0:T(4,128)S(1)}, f32[3,32]{1,0:T(4,128)S(1)}, u32[]{:S(2)}, u32[]{:S(2)}) collective-permute-start(f32[3,32]{1,0:T(4,128)S(1)} %get-tuple-element.45), channel_id=1, source_target_pairs={{0,47},{1,0},{2,1},{3,2},{4,3},{5,4},{6,5},{7,6},{8,7},{9,8},{10,9... | collective-permute-start | bytes 1160 | tf_op jit(solution)/shard_map/ppermute | solution.py:16
  127.6 4.8 %collective-permute-start.21 = (f32[3,32]{1,0:T(4,128)S(1)}, f32[3,32]{1,0:T(4,128)S(1)}, u32[]{:S(2)}, u32[]{:S(2)}) collective-permute-start(f32[3,32]{1,0:T(4,128)S(1)} %get-tuple-element.46), channel_id=1, source_target_pairs={{0,2},{1,3},{2,4},{3,5},{4,6},{5,7},{6,8},{7,9},{8,10},{9,11},{10,... | collective-permute-start | bytes 1160 | tf_op jit(solution)/shard_map/ppermute | solution.py:16
  132.4 1.9 %collective-permute-start.20 = (f32[3,32]{1,0:T(4,128)S(1)}, f32[3,32]{1,0:T(4,128)S(1)}, u32[]{:S(2)}, u32[]{:S(2)}) collective-permute-start(f32[3,32]{1,0:T(4,128)S(1)} %get-tuple-element.43), channel_id=1, source_target_pairs={{0,1},{1,2},{2,3},{3,4},{4,5},{5,6},{6,7},{7,8},{8,9},{9,10},{10,1... | collective-permute-start | bytes 1160 | tf_op jit(solution)/shard_map/ppermute | solution.py:16
  134.3 1.9 %collective-permute-start.19 = (f32[3,32]{1,0:T(4,128)S(1)}, f32[3,32]{1,0:T(4,128)S(1)}, u32[]{:S(2)}, u32[]{:S(2)}) collective-permute-start(f32[3,32]{1,0:T(4,128)S(1)} %get-tuple-element.40), channel_id=1, source_target_pairs={{0,672},{48,720},{96,0},{144,48},{192,96},{240,144},{288,192},{336... | collective-permute-start | bytes 1160 | tf_op jit(solution)/shard_map/ppermute | solution.py:16
  136.3 0.6 convolution_bitcast_fusion.1
  136.8 1.9 %collective-permute-start.18 = (f32[3,32]{1,0:T(4,128)S(1)}, f32[3,32]{1,0:T(4,128)S(1)}, u32[]{:S(2)}, u32[]{:S(2)}) collective-permute-start(f32[3,32]{1,0:T(4,128)S(1)} %get-tuple-element.41), channel_id=1, source_target_pairs={{0,720},{48,0},{96,48},{144,96},{192,144},{240,192},{288,240},{336... | collective-permute-start | bytes 1160 | tf_op jit(solution)/shard_map/ppermute | solution.py:16
  138.8 3.9 %collective-permute-start.17 = (f32[3,32]{1,0:T(4,128)S(1)}, f32[3,32]{1,0:T(4,128)S(1)}, u32[]{:S(2)}, u32[]{:S(2)}) collective-permute-start(f32[3,32]{1,0:T(4,128)S(1)} %get-tuple-element.42), channel_id=1, source_target_pairs={{0,96},{48,144},{96,192},{144,240},{192,288},{240,336},{288,384},{... | collective-permute-start | bytes 1160 | tf_op jit(solution)/shard_map/ppermute | solution.py:16
  142.7 2.1 %collective-permute-start.16 = (f32[3,32]{1,0:T(4,128)S(1)}, f32[3,32]{1,0:T(4,128)S(1)}, u32[]{:S(2)}, u32[]{:S(2)}) collective-permute-start(f32[3,32]{1,0:T(4,128)S(1)} %get-tuple-element.39), channel_id=1, source_target_pairs={{0,48},{48,96},{96,144},{144,192},{192,240},{240,288},{288,336},{3... | collective-permute-start | bytes 1160 | tf_op jit(solution)/shard_map/ppermute | solution.py:16
  144.9 4.0 %collective-permute-start.27 = (f32[32,128]{1,0:T(8,128)S(1)}, f32[32,128]{1,0:T(8,128)S(1)}, u32[]{:S(2)}, u32[]{:S(2)}) collective-permute-start(f32[32,128]{1,0:T(8,128)S(1)} %get-tuple-element.24), channel_id=1, source_target_pairs={{0,672},{48,720},{96,0},{144,48},{192,96},{240,144},{288,192},{336... | collective-permute-start | bytes 49160 | tf_op jit(solution)/shard_map/ppermute | solution.py:16
  148.9 3.4 %collective-permute-start.26 = (f32[32,128]{1,0:T(8,128)S(1)}, f32[32,128]{1,0:T(8,128)S(1)}, u32[]{:S(2)}, u32[]{:S(2)}) collective-permute-start(f32[32,128]{1,0:T(8,128)S(1)} %get-tuple-element.25), channel_id=1, source_target_pairs={{0,720},{48,0},{96,48},{144,96},{192,144},{240,192},{288,240},{336... | collective-permute-start | bytes 49160 | tf_op jit(solution)/shard_map/ppermute | solution.py:16
  152.4 3.6 %collective-permute-start.25 = (f32[32,128]{1,0:T(8,128)S(1)}, f32[32,128]{1,0:T(8,128)S(1)}, u32[]{:S(2)}, u32[]{:S(2)}) collective-permute-start(f32[32,128]{1,0:T(8,128)S(1)} %get-tuple-element.26), channel_id=1, source_target_pairs={{0,96},{48,144},{96,192},{144,240},{192,288},{240,336},{288,384},{... | collective-permute-start | bytes 49160 | tf_op jit(solution)/shard_map/ppermute | solution.py:16
  156.0 1.9 %collective-permute-start.24 = (f32[32,128]{1,0:T(8,128)S(1)}, f32[32,128]{1,0:T(8,128)S(1)}, u32[]{:S(2)}, u32[]{:S(2)}) collective-permute-start(f32[32,128]{1,0:T(8,128)S(1)} %get-tuple-element.23), channel_id=1, source_target_pairs={{0,48},{48,96},{96,144},{144,192},{192,240},{240,288},{288,336},{3... | collective-permute-start | bytes 49160 | tf_op jit(solution)/shard_map/ppermute | solution.py:16
  158.0 0.6 copy.65
  158.6 1.6 collective-permute-done.25
  160.1 3.1 %collective-permute-done.24 = f32[32,128]{1,0:T(8,128)S(1)} collective-permute-done((f32[32,128]{1,0:T(8,128)S(1)}, f32[32,128]{1,0:T(8,128)S(1)}, u32[]{:S(2)}, u32[]{:S(2)}) %collective-permute-start.24) | collective-permute-done | bytes 16416 | tf_op jit(solution)/shard_map/ppermute | solution.py:16
  163.2 0.6 fusion.64
  (111 shorter events, 3.5 us)
Async XLA Ops:
  0.6 64.2 %copy-start = (f32[32,384]{1,0:T(8,128)S(1)}, f32[32,384]{1,0:T(8,128)}, u32[]{:S(2)}) copy-start(f32[32,384]{1,0:T(8,128)} %param.19) | copy-start | bytes 147460
  1.3 25.9 %collective-permute-start.4 = (f32[3,32]{1,0:T(4,128)S(1)}, f32[3,32]{1,0:T(4,128)S(1)}, u32[]{:S(2)}, u32[]{:S(2)}) collective-permute-start(f32[3,32]{1,0:T(4,128)S(1)} %bitcast.270), channel_id=1, source_target_pairs={{0,2},{1,3},{2,4},{3,5},{4,6},{5,7},{6,8},{7,9},{8,10},{9,11},{10,... | collective-permute-start | bytes 1160 | tf_op jit(solution)/shard_map/ppermute | solution.py:16
  7.4 33.2 %collective-permute-start.5 = (f32[3,32]{1,0:T(4,128)S(1)}, f32[3,32]{1,0:T(4,128)S(1)}, u32[]{:S(2)}, u32[]{:S(2)}) collective-permute-start(f32[3,32]{1,0:T(4,128)S(1)} %bitcast.271), channel_id=1, source_target_pairs={{0,1},{1,2},{2,3},{3,4},{4,5},{5,6},{6,7},{7,8},{8,9},{9,10},{10,1... | collective-permute-start | bytes 1160 | tf_op jit(solution)/shard_map/ppermute | solution.py:16
  11.7 18.0 %collective-permute-start = (f32[3,32]{1,0:T(4,128)S(1)}, f32[3,32]{1,0:T(4,128)S(1)}, u32[]{:S(2)}, u32[]{:S(2)}) collective-permute-start(f32[3,32]{1,0:T(4,128)S(1)} %bitcast.272), channel_id=1, source_target_pairs={{0,96},{48,144},{96,192},{144,240},{192,288},{240,336},{288,384},{... | collective-permute-start | bytes 1160 | tf_op jit(solution)/shard_map/ppermute | solution.py:16
  15.1 30.4 %collective-permute-start.1 = (f32[3,32]{1,0:T(4,128)S(1)}, f32[3,32]{1,0:T(4,128)S(1)}, u32[]{:S(2)}, u32[]{:S(2)}) collective-permute-start(f32[3,32]{1,0:T(4,128)S(1)} %bitcast.273), channel_id=1, source_target_pairs={{0,48},{48,96},{96,144},{144,192},{192,240},{240,288},{288,336},{3... | collective-permute-start | bytes 1160 | tf_op jit(solution)/shard_map/ppermute | solution.py:16
  17.0 32.6 %collective-permute-start.2 = (f32[3,32]{1,0:T(4,128)S(1)}, f32[3,32]{1,0:T(4,128)S(1)}, u32[]{:S(2)}, u32[]{:S(2)}) collective-permute-start(f32[3,32]{1,0:T(4,128)S(1)} %bitcast.274), channel_id=1, source_target_pairs={{0,720},{48,0},{96,48},{144,96},{192,144},{240,192},{288,240},{336... | collective-permute-start | bytes 1160 | tf_op jit(solution)/shard_map/ppermute | solution.py:16
  25.1 41.0 %copy-start.18 = (f32[8]{0:T(128)}, f32[8]{0:T(128)S(1)}, u32[]{:S(2)}) copy-start(f32[8]{0:T(128)S(1)} %convert_multiply_fusion) | copy-start | bytes 100
  25.8 37.2 %copy-start.2 = (s32[1,1,5,5,32]{4,3,1,2,0:T(8,128)}, s32[1,1,5,5,32]{4,3,1,2,0:T(8,128)S(1)}, u32[]{:S(2)}) copy-start(s32[1,1,5,5,32]{4,3,1,2,0:T(8,128)S(1)} %copy.117) | copy-start | bytes 9604
  26.5 36.4 %copy-start.9 = (s32[1,1,5,5,32]{4,3,1,2,0:T(8,128)}, s32[1,1,5,5,32]{4,3,1,2,0:T(8,128)S(1)}, u32[]{:S(2)}) copy-start(s32[1,1,5,5,32]{4,3,1,2,0:T(8,128)S(1)} %copy.116) | copy-start | bytes 9604
  27.3 35.7 %copy-start.5 = (f32[1,1,5,5,32]{4,1,3,2,0:T(1,128)}, f32[1,1,5,5,32]{4,1,3,2,0:T(1,128)S(1)}, u32[]{:S(2)}) copy-start(f32[1,1,5,5,32]{4,1,3,2,0:T(1,128)S(1)} %convert_element_type.37) | copy-start | bytes 9604
  27.3 24.3 %collective-permute-start.3 = (f32[3,32]{1,0:T(4,128)S(1)}, f32[3,32]{1,0:T(4,128)S(1)}, u32[]{:S(2)}, u32[]{:S(2)}) collective-permute-start(f32[3,32]{1,0:T(4,128)S(1)} %bitcast.275), channel_id=1, source_target_pairs={{0,672},{48,720},{96,0},{144,48},{192,96},{240,144},{288,192},{336... | collective-permute-start | bytes 1160 | tf_op jit(solution)/shard_map/ppermute | solution.py:16
  29.8 27.8 %collective-permute-start.6 = (f32[3,32]{1,0:T(4,128)S(1)}, f32[3,32]{1,0:T(4,128)S(1)}, u32[]{:S(2)}, u32[]{:S(2)}) collective-permute-start(f32[3,32]{1,0:T(4,128)S(1)} %bitcast.276), channel_id=1, source_target_pairs={{0,47},{1,0},{2,1},{3,2},{4,3},{5,4},{6,5},{7,6},{8,7},{9,8},{10,9... | collective-permute-start | bytes 1160 | tf_op jit(solution)/shard_map/ppermute | solution.py:16
  40.6 19.4 %collective-permute-start.7 = (f32[3,32]{1,0:T(4,128)S(1)}, f32[3,32]{1,0:T(4,128)S(1)}, u32[]{:S(2)}, u32[]{:S(2)}) collective-permute-start(f32[3,32]{1,0:T(4,128)S(1)} %bitcast.277), channel_id=1, source_target_pairs={{0,46},{1,47},{2,0},{3,1},{4,2},{5,3},{6,4},{7,5},{8,6},{9,7},{10,... | collective-permute-start | bytes 1160 | tf_op jit(solution)/shard_map/ppermute | solution.py:16
  45.5 25.2 %collective-permute-start.12 = (f32[32,128]{1,0:T(8,128)}, f32[32,128]{1,0:T(8,128)}, u32[]{:S(2)}, u32[]{:S(2)}) collective-permute-start(f32[32,128]{1,0:T(8,128)} %bitcast.265), channel_id=1, source_target_pairs={{0,96},{48,144},{96,192},{144,240},{192,288},{240,336},{288,384},{... | collective-permute-start | bytes 49160 | tf_op jit(solution)/shard_map/ppermute | solution.py:16
  49.6 24.2 %collective-permute-start.13 = (f32[32,128]{1,0:T(8,128)}, f32[32,128]{1,0:T(8,128)}, u32[]{:S(2)}, u32[]{:S(2)}) collective-permute-start(f32[32,128]{1,0:T(8,128)} %bitcast.266), channel_id=1, source_target_pairs={{0,48},{48,96},{96,144},{144,192},{192,240},{240,288},{288,336},{3... | collective-permute-start | bytes 49160 | tf_op jit(solution)/shard_map/ppermute | solution.py:16
  51.5 30.6 %collective-permute-start.14 = (f32[32,128]{1,0:T(8,128)}, f32[32,128]{1,0:T(8,128)}, u32[]{:S(2)}, u32[]{:S(2)}) collective-permute-start(f32[32,128]{1,0:T(8,128)} %bitcast.267), channel_id=1, source_target_pairs={{0,720},{48,0},{96,48},{144,96},{192,144},{240,192},{288,240},{336... | collective-permute-start | bytes 49160 | tf_op jit(solution)/shard_map/ppermute | solution.py:16
  57.6 30.3 %collective-permute-start.15 = (f32[32,128]{1,0:T(8,128)}, f32[32,128]{1,0:T(8,128)}, u32[]{:S(2)}, u32[]{:S(2)}) collective-permute-start(f32[32,128]{1,0:T(8,128)} %bitcast.268), channel_id=1, source_target_pairs={{0,672},{48,720},{96,0},{144,48},{192,96},{240,144},{288,192},{336... | collective-permute-start | bytes 49160 | tf_op jit(solution)/shard_map/ppermute | solution.py:16
  60.1 29.8 %collective-permute-start.8 = (f32[32,1152]{1,0:T(8,128)}, f32[32,1152]{1,0:T(8,128)}, u32[]{:S(2)}, u32[]{:S(2)}) collective-permute-start(f32[32,1152]{1,0:T(8,128)} %bitcast.257), channel_id=1, source_target_pairs={{0,2},{1,3},{2,4},{3,5},{4,6},{5,7},{6,8},{7,9},{8,10},{9,11},{10,... | collective-permute-start | bytes 442376 | tf_op jit(solution)/shard_map/ppermute | solution.py:16
  62.3 4.3 %copy-start.13 = (f32[5,5,32]{2,1,0:T(8,128)}, f32[5,5,32]{2,1,0:T(8,128)S(1)}, u32[]{:S(2)}) copy-start(f32[5,5,32]{2,1,0:T(8,128)S(1)} %get-tuple-element.49) | copy-start | bytes 9604
  62.9 3.7 %copy-start.11 = (f32[5,5,32]{2,1,0:T(8,128)}, f32[5,5,32]{2,1,0:T(8,128)S(1)}, u32[]{:S(2)}) copy-start(f32[5,5,32]{2,1,0:T(8,128)S(1)} %get-tuple-element.36) | copy-start | bytes 9604
  62.9 3.7 %copy-start.7 = (f32[5,5,32]{2,1,0:T(8,128)}, f32[5,5,32]{2,1,0:T(8,128)S(1)}, u32[]{:S(2)}) copy-start(f32[5,5,32]{2,1,0:T(8,128)S(1)} %get-tuple-element.37) | copy-start | bytes 9604
  67.7 14.4 %copy-start.16 = (f32[1,1,32,128]{3,2,1,0:T(8,128)S(1)}, f32[1,1,32,128]{3,2,1,0:T(8,128)}, u32[]{:S(2)}) copy-start(f32[1,1,32,128]{3,2,1,0:T(8,128)} %param.11) | copy-start | bytes 49156
  70.6 20.1 %collective-permute-start.9 = (f32[32,1152]{1,0:T(8,128)}, f32[32,1152]{1,0:T(8,128)S(1)}, u32[]{:S(2)}, u32[]{:S(2)}) collective-permute-start(f32[32,1152]{1,0:T(8,128)} %bitcast.258), channel_id=1, source_target_pairs={{0,1},{1,2},{2,3},{3,4},{4,5},{5,6},{6,7},{7,8},{8,9},{9,10},{10,1... | collective-permute-start | bytes 442376 | tf_op jit(solution)/shard_map/ppermute | solution.py:16
  73.8 17.9 %collective-permute-start.10 = (f32[32,1152]{1,0:T(8,128)}, f32[32,1152]{1,0:T(8,128)S(1)}, u32[]{:S(2)}, u32[]{:S(2)}) collective-permute-start(f32[32,1152]{1,0:T(8,128)} %bitcast.259), channel_id=1, source_target_pairs={{0,47},{1,0},{2,1},{3,2},{4,3},{5,4},{6,5},{7,6},{8,7},{9,8},{10,9... | collective-permute-start | bytes 442376 | tf_op jit(solution)/shard_map/ppermute | solution.py:16
  82.2 10.2 %collective-permute-start.11 = (f32[32,1152]{1,0:T(8,128)}, f32[32,1152]{1,0:T(8,128)S(1)}, u32[]{:S(2)}, u32[]{:S(2)}) collective-permute-start(f32[32,1152]{1,0:T(8,128)} %bitcast.260), channel_id=1, source_target_pairs={{0,46},{1,47},{2,0},{3,1},{4,2},{5,3},{6,4},{7,5},{8,6},{9,7},{10,... | collective-permute-start | bytes 442376 | tf_op jit(solution)/shard_map/ppermute | solution.py:16
  106.6 1.3 copy-start.1
  108.6 0.7 copy-start.4
  108.6 0.9 copy-start.8
  110.8 0.7 copy-start.12
  110.8 0.7 copy-start.15
  110.8 0.7 copy-start.17
  110.8 0.7 copy-start.19
  111.0 2.4 %copy-start.6 = (f32[1,1,5,5,32]{4,1,3,2,0:T(1,128)S(1)}, f32[1,1,5,5,32]{4,1,3,2,0:T(1,128)}, u32[]{:S(2)}) copy-start(f32[1,1,5,5,32]{4,1,3,2,0:T(1,128)} %copy-done.5) | copy-start | bytes 9604
  111.0 2.4 %copy-start.14 = (f32[5,5,32]{2,1,0:T(8,128)S(1)}, f32[5,5,32]{2,1,0:T(8,128)}, u32[]{:S(2)}) copy-start(f32[5,5,32]{2,1,0:T(8,128)} %copy-done.13) | copy-start | bytes 9604
  111.5 2.1 %copy-start.10 = (s32[1,1,5,5,32]{4,3,1,2,0:T(8,128)S(1)}, s32[1,1,5,5,32]{4,3,1,2,0:T(8,128)}, u32[]{:S(2)}) copy-start(s32[1,1,5,5,32]{4,3,1,2,0:T(8,128)} %copy-done.9) | copy-start | bytes 9604
  111.5 2.5 %copy-start.3 = (s32[1,1,5,5,32]{4,3,1,2,0:T(8,128)S(1)}, s32[1,1,5,5,32]{4,3,1,2,0:T(8,128)}, u32[]{:S(2)}) copy-start(s32[1,1,5,5,32]{4,3,1,2,0:T(8,128)} %copy-done.2) | copy-start | bytes 9604
  114.4 22.5 %collective-permute-start.23 = (f32[3,32]{1,0:T(4,128)S(1)}, f32[3,32]{1,0:T(4,128)S(1)}, u32[]{:S(2)}, u32[]{:S(2)}) collective-permute-start(f32[3,32]{1,0:T(4,128)S(1)} %get-tuple-element.44), channel_id=1, source_target_pairs={{0,46},{1,47},{2,0},{3,1},{4,2},{5,3},{6,4},{7,5},{8,6},{9,7},{10,... | collective-permute-start | bytes 1160 | tf_op jit(solution)/shard_map/ppermute | solution.py:16
  124.2 14.5 %collective-permute-start.22 = (f32[3,32]{1,0:T(4,128)S(1)}, f32[3,32]{1,0:T(4,128)S(1)}, u32[]{:S(2)}, u32[]{:S(2)}) collective-permute-start(f32[3,32]{1,0:T(4,128)S(1)} %get-tuple-element.45), channel_id=1, source_target_pairs={{0,47},{1,0},{2,1},{3,2},{4,3},{5,4},{6,5},{7,6},{8,7},{9,8},{10,9... | collective-permute-start | bytes 1160 | tf_op jit(solution)/shard_map/ppermute | solution.py:16
  127.6 15.1 %collective-permute-start.21 = (f32[3,32]{1,0:T(4,128)S(1)}, f32[3,32]{1,0:T(4,128)S(1)}, u32[]{:S(2)}, u32[]{:S(2)}) collective-permute-start(f32[3,32]{1,0:T(4,128)S(1)} %get-tuple-element.46), channel_id=1, source_target_pairs={{0,2},{1,3},{2,4},{3,5},{4,6},{5,7},{6,8},{7,9},{8,10},{9,11},{10,... | collective-permute-start | bytes 1160 | tf_op jit(solution)/shard_map/ppermute | solution.py:16
  132.4 12.5 %collective-permute-start.20 = (f32[3,32]{1,0:T(4,128)S(1)}, f32[3,32]{1,0:T(4,128)S(1)}, u32[]{:S(2)}, u32[]{:S(2)}) collective-permute-start(f32[3,32]{1,0:T(4,128)S(1)} %get-tuple-element.43), channel_id=1, source_target_pairs={{0,1},{1,2},{2,3},{3,4},{4,5},{5,6},{6,7},{7,8},{8,9},{9,10},{10,1... | collective-permute-start | bytes 1160 | tf_op jit(solution)/shard_map/ppermute | solution.py:16
  134.3 14.6 %collective-permute-start.19 = (f32[3,32]{1,0:T(4,128)S(1)}, f32[3,32]{1,0:T(4,128)S(1)}, u32[]{:S(2)}, u32[]{:S(2)}) collective-permute-start(f32[3,32]{1,0:T(4,128)S(1)} %get-tuple-element.40), channel_id=1, source_target_pairs={{0,672},{48,720},{96,0},{144,48},{192,96},{240,144},{288,192},{336... | collective-permute-start | bytes 1160 | tf_op jit(solution)/shard_map/ppermute | solution.py:16
  136.8 15.5 %collective-permute-start.18 = (f32[3,32]{1,0:T(4,128)S(1)}, f32[3,32]{1,0:T(4,128)S(1)}, u32[]{:S(2)}, u32[]{:S(2)}) collective-permute-start(f32[3,32]{1,0:T(4,128)S(1)} %get-tuple-element.41), channel_id=1, source_target_pairs={{0,720},{48,0},{96,48},{144,96},{192,144},{240,192},{288,240},{336... | collective-permute-start | bytes 1160 | tf_op jit(solution)/shard_map/ppermute | solution.py:16
  138.8 17.2 %collective-permute-start.17 = (f32[3,32]{1,0:T(4,128)S(1)}, f32[3,32]{1,0:T(4,128)S(1)}, u32[]{:S(2)}, u32[]{:S(2)}) collective-permute-start(f32[3,32]{1,0:T(4,128)S(1)} %get-tuple-element.42), channel_id=1, source_target_pairs={{0,96},{48,144},{96,192},{144,240},{192,288},{240,336},{288,384},{... | collective-permute-start | bytes 1160 | tf_op jit(solution)/shard_map/ppermute | solution.py:16
  142.7 15.2 %collective-permute-start.16 = (f32[3,32]{1,0:T(4,128)S(1)}, f32[3,32]{1,0:T(4,128)S(1)}, u32[]{:S(2)}, u32[]{:S(2)}) collective-permute-start(f32[3,32]{1,0:T(4,128)S(1)} %get-tuple-element.39), channel_id=1, source_target_pairs={{0,48},{48,96},{96,144},{144,192},{192,240},{240,288},{288,336},{3... | collective-permute-start | bytes 1160 | tf_op jit(solution)/shard_map/ppermute | solution.py:16
  144.9 13.7 %collective-permute-start.27 = (f32[32,128]{1,0:T(8,128)S(1)}, f32[32,128]{1,0:T(8,128)S(1)}, u32[]{:S(2)}, u32[]{:S(2)}) collective-permute-start(f32[32,128]{1,0:T(8,128)S(1)} %get-tuple-element.24), channel_id=1, source_target_pairs={{0,672},{48,720},{96,0},{144,48},{192,96},{240,144},{288,192},{336... | collective-permute-start | bytes 49160 | tf_op jit(solution)/shard_map/ppermute | solution.py:16
  148.9 9.6 %collective-permute-start.26 = (f32[32,128]{1,0:T(8,128)S(1)}, f32[32,128]{1,0:T(8,128)S(1)}, u32[]{:S(2)}, u32[]{:S(2)}) collective-permute-start(f32[32,128]{1,0:T(8,128)S(1)} %get-tuple-element.25), channel_id=1, source_target_pairs={{0,720},{48,0},{96,48},{144,96},{192,144},{240,192},{288,240},{336... | collective-permute-start | bytes 49160 | tf_op jit(solution)/shard_map/ppermute | solution.py:16
  152.4 7.7 %collective-permute-start.25 = (f32[32,128]{1,0:T(8,128)S(1)}, f32[32,128]{1,0:T(8,128)S(1)}, u32[]{:S(2)}, u32[]{:S(2)}) collective-permute-start(f32[32,128]{1,0:T(8,128)S(1)} %get-tuple-element.26), channel_id=1, source_target_pairs={{0,96},{48,144},{96,192},{144,240},{192,288},{240,336},{288,384},{... | collective-permute-start | bytes 49160 | tf_op jit(solution)/shard_map/ppermute | solution.py:16
  156.0 7.2 %collective-permute-start.24 = (f32[32,128]{1,0:T(8,128)S(1)}, f32[32,128]{1,0:T(8,128)S(1)}, u32[]{:S(2)}, u32[]{:S(2)}) collective-permute-start(f32[32,128]{1,0:T(8,128)S(1)} %get-tuple-element.23), channel_id=1, source_target_pairs={{0,48},{48,96},{96,144},{144,192},{192,240},{240,288},{288,336},{3... | collective-permute-start | bytes 49160 | tf_op jit(solution)/shard_map/ppermute | solution.py:16
where the time goes:
time: 166 us; the launch traced here: 164 us
  starting transfers between devices  113 us (68%)
  local copies, waits for them, and re-layouts  19 us (11%)
  matrix products  14.7 us (9%)
  other arithmetic  10.3 us (6%)
  waiting for transfers between devices  5.34 us (3%)
    ppermute x28, starting transfers between devices, shifted(): lax.ppermute(value, axis, [(i, (i + by) % peers) for i in range(peers)])  113 us
    unnamed x61, local copies, waits for them, and re-layouts  9.47 us
    reshape x1, local copies, waits for them, and re-layouts, tile_grads(): jnp.dot(tgt_onehot, cot_block, precision=highest)  5.84 us
    ppermute x28, waiting for transfers between devices, shifted(): lax.ppermute(value, axis, [(i, (i + by) % peers) for i in range(peers)])  5.34 us
    dot_general x1, matrix products, tile_grads(): jnp.dot(tgt_onehot, cot_block, precision=highest)  4.24 us
    mul x1, other arithmetic, tile_grads(): weighted = gathered_cot * gathered_feats[:, None, :]  4.08 us
    dot_general x2, matrix products, tile_geometry(): jnp.dot(radial_basis, w_in, precision=highest)  3.7 us
  transfers between devices with their start and end apart: 28, of which 3 were waited for; matrix products, arithmetic and copies ran while one was open for 13% of the time, Pallas kernels for 0%

commit v1 on v0

v1 whole, which is shorter than its diff:
```python
import math

import jax
import jax.numpy as jnp
from jax import lax
from jax.experimental import pallas as pl
from jax.experimental.pallas import tpu as pltpu
from jax.sharding import PartitionSpec as P

MESH = pl.DeviceIdType.MESH
SIDE = 5.0
CUTOFF = 12.0
SOFTEN = 0.25
LANES = 256
F32 = jnp.float32
BF16 = jnp.bfloat16
NN = (((1,), (0,)), ((), ()))
NT = (((1,), (1,)), ((), ()))
TN = (((0,), (0,)), ((), ()))
HIGHEST = lax.Precision.HIGHEST
STEPS = (-2, -1, 0, 1, 2)
AWAY = (-1, 1, -2, 2)


def dot(lhs, rhs, dims):
    return lax.dot_general(lhs, rhs, dims, preferred_element_type=F32)


def exact_dot(lhs, rhs, dims):
    return lax.dot_general(lhs, rhs, dims, precision=HIGHEST, preferred_element_type=F32)


def split2(value):
    high = value.astype(BF16).astype(F32)
    return high, value - high


def split3(value):
    high, rest = split2(value)
    middle, low = split2(rest)
    return high, middle, low


def sin_cos_pi(x):
    turns = jnp.floor(x + 0.5)
    y = (x - turns) * math.pi
    half = turns * 0.5
    sign = 1.0 - 4.0 * (half - jnp.floor(half))
    y2 = y * y
    s = -1.0 / 39916800.0 + y2 * (1.0 / 6227020800.0)
    for c in (1.0 / 362880.0, -1.0 / 5040.0, 1.0 / 120.0, -1.0 / 6.0, 1.0):
        s = s * y2 + c
    c_ = 1.0 / 479001600.0 - y2 * (1.0 / 87178291200.0)
    for c in (-1.0 / 3628800.0, 1.0 / 40320.0, -1.0 / 720.0, 1.0 / 24.0, -0.5, 1.0):
        c_ = c_ * y2 + c
    return s * y * sign, c_ * sign


def kernel(
    pos_in, feat_in, cot_in, src_in, tgt_in, mask_in, spec_in, w_in, emb, w_out,
    pos_out, feat_out,
    posx, posy, feats, cots, lists, index, posmat, onehot, gath, fbuf, radial, wt, featt,
    sph, rows, pp, acc, tgt_send, ret, tgt_ret,
    local_sem, fx_send, fx_recv, py_send, py_recv, px_send, px_recv, ct_send, ct_recv,
    rs_send, rs_recv, rt_send, rt_recv,
):
    a, b = lax.axis_index("gx"), lax.axis_index("gy")
    na, nb = lax.axis_size("gx"), lax.axis_size("gy")
    along_x = {s: (lax.rem(a + s + na, na), b) for s in STEPS}
    along_y = {s: (a, lax.rem(b + s + nb, nb)) for s in STEPS}

    barrier = pltpu.get_barrier_semaphore()
    for s in AWAY:
        pl.semaphore_signal(barrier, inc=1, device_id=along_x[s], device_id_type=MESH)
        pl.semaphore_signal(barrier, inc=1, device_id=along_y[s], device_id_type=MESH)

    own = [
        pltpu.make_async_copy(src_in.at[0, 0], lists.at[0], local_sem.at[0]),
        pltpu.make_async_copy(tgt_in.at[0, 0], lists.at[1], local_sem.at[1]),
        pltpu.make_async_copy(mask_in.at[0, 0], lists.at[2], local_sem.at[2]),
        pltpu.make_async_copy(spec_in.at[0, 0], lists.at[3], local_sem.at[3]),
        pltpu.make_async_copy(pos_in.at[0, 0], posx.at[2], local_sem.at[4]),
        pltpu.make_async_copy(pos_in.at[0, 0], posy.at[2], local_sem.at[5]),
        pltpu.make_async_copy(feat_in.at[0, 0], feats.at[2], local_sem.at[6]),
        pltpu.make_async_copy(cot_in.at[0, 0], cots.at[2], local_sem.at[7]),
    ]
    for copy in own:
        copy.start()

    pl.semaphore_wait(barrier, 8)

    def send(src, dst, send_sem, recv_sem, device):
        copy = pltpu.make_async_remote_copy(
            src_ref=src, dst_ref=dst, send_sem=send_sem, recv_sem=recv_sem, device_id=device, device_id_type=MESH
        )
        copy.start()
        return copy

    sent_px, sent_py, sent_fx, sent_ct = {}, {}, {}, {}
    for s in AWAY:
        i = s + 2
        sent_px[s] = send(pos_in.at[0, 0], posx.at[i], px_send.at[i], px_recv.at[i], along_x[-s])
        sent_py[s] = send(pos_in.at[0, 0], posy.at[i], py_send.at[i], py_recv.at[i], along_y[-s])
    for s in AWAY:
        i = s + 2
        sent_ct[s] = send(cot_in.at[0, 0], cots.at[i], ct_send.at[i], ct_recv.at[i], along_y[-s])
        sent_fx[s] = send(feat_in.at[0, 0], feats.at[i], fx_send.at[i], fx_recv.at[i], along_x[-s])

    for copy in own:
        copy.wait()
    index[...] = jnp.zeros_like(index)
    for i in range(5):
        for field in range(4):
            index[field, 0:5, 32 * i : 32 * i + 32] = lists[field, i]
    lane = lax.broadcasted_iota(jnp.int32, (8, LANES), 1)
    group = lane // 32
    src_rows = jnp.where(lane < 160, index[0] + 32 * group, -1)
    tgt_rows = jnp.where(lane < 160, index[1] + 160, -1)
    alive = index[2].astype(F32)
    species = index[3]

    src_ids = lax.broadcasted_iota(jnp.int32, (160, LANES), 0)
    tgt_ids = lax.broadcasted_iota(jnp.int32, (32, LANES), 0) + 160
    for j in range(5):
        onehot[j, 0:160] = (src_ids == src_rows[j : j + 1]).astype(F32).astype(BF16)
        onehot[j, 160:192] = (tgt_ids == tgt_rows[j : j + 1]).astype(F32).astype(BF16)

    w_high, w_low = split2(w_out[...])
    wt[...] = jnp.concatenate([w_high, w_high, w_low], axis=0).T.astype(BF16)

    for s in AWAY:
        sent_px[s].wait_recv()
        sent_py[s].wait_recv()
    posmat[...] = jnp.zeros_like(posmat)
    for i in range(5):
        posmat[0:3, 32 * i : 32 * i + 32] = posx[i]
    rel = []
    for j in range(5):
        posmat[0:3, 160:192] = -posy[j]
        pieces = jnp.concatenate(split3(posmat[...]), axis=0).astype(BF16)
        picked = dot(pieces, onehot[j], NN)
        rel.append(picked[0:8] + picked[8:16] + picked[16:24])
    step_row = lax.broadcasted_iota(jnp.int32, (8, LANES), 0)
    pad = [jnp.zeros((1, LANES), F32)] * 3
    rx = jnp.concatenate([r[0:1] for r in rel] + pad, axis=0) + (group - 2).astype(F32) * SIDE
    ry = jnp.concatenate([r[1:2] for r in rel] + pad, axis=0) - (step_row - 2).astype(F32) * SIDE
    rz = jnp.concatenate([r[2:3] for r in rel] + pad, axis=0)
    dist = jnp.sqrt(rx * rx + ry * ry + rz * rz + SOFTEN)
    inv = 1.0 / dist
    ux, uy, uz = rx * inv, ry * inv, rz * inv
    q = dist * (1.0 / CUTOFF)
    left = jnp.maximum(1.0 - q * q, 0.0)
    env = left * left * alive
    denv = q * left * alive * (-4.0 / CUTOFF)
    r3, r5, r15 = math.sqrt(3.0), math.sqrt(5.0), math.sqrt(15.0)
    for m, y in enumerate(
        (
            r3 * ux, r3 * uy, r3 * uz,
            r15 * ux * uy, r15 * uy * uz, 0.5 * r5 * (2.0 * uz * uz - ux * ux - uy * uy),
            r15 * ux * uz, 0.5 * r15 * (ux * ux - uy * uy),
        )
    ):
        sph[m] = y
    for k, value in enumerate((ux, uy, uz, inv)):
        rows[k] = value

    order = (lax.broadcasted_iota(jnp.int32, (8, LANES), 0) + 1).astype(F32)
    spec_ids = lax.broadcasted_iota(jnp.int32, (10, LANES), 0)
    root = math.sqrt(2.0 / CUTOFF)
    for j in range(5):
        inv_j, env_j, denv_j = inv[j : j + 1], env[j : j + 1], denv[j : j + 1]
        sine, cosine = sin_cos_pi(order * q[j : j + 1])
        basis = root * sine * inv_j
        dbasis = (order * (root * math.pi / CUTOFF) * cosine - basis) * inv_j
        chosen = (spec_ids == species[j : j + 1]).astype(F32)
        both = exact_dot(w_in[...], jnp.concatenate([basis, dbasis], axis=1), TN)
        z = both[:, 0:LANES] + exact_dot(emb[...], chosen, TN)
        dz = both[:, LANES:]
        sig = 1.0 / (1.0 + jnp.exp(-z))
        hidden = z * sig
        dhidden = sig * (1.0 + z * (1.0 - sig)) * dz
        stacked = jnp.concatenate([hidden * env_j, dhidden * env_j + hidden * denv_j], axis=1)
        high, low = split2(stacked)
        radial[j] = dot(wt[...], jnp.concatenate([high, low, high], axis=0).astype(BF16), NN)

    for s in AWAY:
        sent_fx[s].wait_recv()
    all_feats = jnp.concatenate([feats[i] for i in range(5)], axis=0)
    f_high, f_low = split2(all_feats)
    featt[...] = jnp.concatenate([f_high, f_low], axis=1).T.astype(BF16)
    for j in range(5):
        two = dot(featt[...], onehot[j, 0:160], NN)
        fbuf[j] = two[0:128] + two[128:256]

    acc[...] = jnp.zeros_like(acc)

    for s in (0, -1, 1, -2, 2):
        j = s + 2
        if s != 0:
            sent_ct[s].wait_recv()
        c_high, c_low = split2(cots[j])
        target_hot = onehot[j, 160:192]
        gath[...] = dot(
            jnp.concatenate([c_high, c_low], axis=0).astype(BF16).T, jnp.concatenate([target_hot, target_hot], axis=0), NN
        )

        def channels(c, carry, j=j):
            r0 = pl.multiple_of(c * 8, 8)
            f = fbuf[j, pl.ds(r0, 8), :]
            g = [gath[pl.ds(m * 128 + r0, 8), :] for m in range(9)]
            y = [None] + [sph[m, j : j + 1, :] for m in range(8)]
            rad = [radial[j, pl.ds(l * 128 + r0, 8), 0:LANES] for l in range(3)]
            drad = [radial[j, pl.ds(l * 128 + r0, 8), LANES : 2 * LANES] for l in range(3)]
            c1 = y[1] * g[1] + y[2] * g[2] + y[3] * g[3]
            c2 = y[4] * g[4] + y[5] * g[5] + y[6] * g[6] + y[7] * g[7] + y[8] * g[8]
            pp[pl.ds(r0, 8), :] = rad[0] * g[0] + rad[1] * c1 + rad[2] * c2
            p1, p2 = rad[1] * f, rad[2] * f
            out = [carry[0] + f * (drad[0] * g[0] + drad[1] * c1 + drad[2] * c2)]
            for m in range(1, 9):
                out.append(carry[m] + (p1 if m < 4 else p2) * g[m])
            return tuple(out)

        start = tuple(jnp.zeros((8, LANES), F32) for _ in range(9))
        sums = lax.fori_loop(0, 16, channels, start)
        gd, *gy = [jnp.sum(v, axis=0, keepdims=True) for v in sums]
        ux_j, uy_j, uz_j, inv_j = (rows[k, j : j + 1, :] for k in range(4))
        gux = r3 * gy[0] + r15 * (uy_j * gy[3] + uz_j * gy[6] + ux_j * gy[7]) - r5 * ux_j * gy[5]
        guy = r3 * gy[1] + r15 * (ux_j * gy[3] + uz_j * gy[4] - uy_j * gy[7]) - r5 * uy_j * gy[5]
        guz = r3 * gy[2] + r15 * (uy_j * gy[4] + ux_j * gy[6]) + 2.0 * r5 * uz_j * gy[5]
        along = gd - (gux * ux_j + guy * uy_j + guz * uz_j) * inv_j
        grad = jnp.concatenate(
            [gux * inv_j + along * ux_j, guy * inv_j + along * uy_j, guz * inv_j + along * uz_j]
            + [jnp.zeros((5, LANES), F32)],
            axis=0,
        )
        scat = dot(jnp.concatenate(split2(grad), axis=0).astype(BF16), onehot[j], NT)
        scat = scat[0:8] + scat[8:16]
        p_high, p_low = split2(pp[...])
        fscat = dot(onehot[j, 0:160], jnp.concatenate([p_high, p_low], axis=0).astype(BF16), NT)
        fscat = fscat[:, 0:128] + fscat[:, 128:256]
        for i in range(5):
            acc[i, 0:32, :] += fscat[32 * i : 32 * i + 32]
            acc[i, 32:40, 0:32] += scat[:, 32 * i : 32 * i + 32]
        tgt_send[j, :, 0:32] = -scat[:, 160:192]

    sent_rs, sent_rt = {}, {}
    for s in AWAY:
        i = s + 2
        sent_rt[s] = send(tgt_send.at[i], tgt_ret.at[i], rt_send.at[i], rt_recv.at[i], along_y[s])
        sent_rs[s] = send(acc.at[i], ret.at[i], rs_send.at[i], rs_recv.at[i], along_x[s])

    pos_total = acc[2, 32:40, :] + tgt_send[2]
    feat_total = acc[2, 0:32, :]
    for s in AWAY:
        i = s + 2
        sent_rs[s].wait_recv()
        feat_total = feat_total + ret[i, 0:32, :]
        pos_total = pos_total + ret[i, 32:40, :]
    feat_out[0, 0] = feat_total
    for s in AWAY:
        sent_rt[s].wait_recv()
        pos_total = pos_total + tgt_ret[s + 2]
    pos_out[0, 0] = pos_total[0:3, 0:32]
    for s in AWAY:
        for sent in (sent_px, sent_py, sent_fx, sent_ct, sent_rs, sent_rt):
            sent[s].wait_send()


def local(positions, features, cotangent, nbr_src, nbr_tgt, pair_mask, pair_species, w_in, species_emb, w_out):
    hbm = pl.BlockSpec(memory_space=pl.ANY)
    vmem = pl.BlockSpec(memory_space=pltpu.VMEM)
    dma = pltpu.SemaphoreType.DMA
    return pl.pallas_call(
        kernel,
        out_shape=(
            jax.ShapeDtypeStruct(positions.shape, F32),
            jax.ShapeDtypeStruct(features.shape, F32),
        ),
        in_specs=[hbm] * 7 + [vmem] * 3,
        out_specs=(vmem, vmem),
        scratch_shapes=[
            pltpu.VMEM((5, 3, 32), F32),
            pltpu.VMEM((5, 3, 32), F32),
            pltpu.VMEM((5, 32, 128), F32),
            pltpu.VMEM((5, 32, 1152), F32),
            pltpu.VMEM((4, 5, 5, 32), jnp.int32),
            pltpu.VMEM((4, 8, LANES), jnp.int32),
            pltpu.VMEM((8, 192), F32),
            pltpu.VMEM((5, 192, LANES), BF16),
            pltpu.VMEM((1152, LANES), F32),
            pltpu.VMEM((5, 128, LANES), F32),
            pltpu.VMEM((5, 384, 2 * LANES), F32),
            pltpu.VMEM((384, 96), BF16),
            pltpu.VMEM((256, 160), BF16),
            pltpu.VMEM((8, 8, LANES), F32),
            pltpu.VMEM((4, 8, LANES), F32),
            pltpu.VMEM((128, LANES), F32),
            pltpu.VMEM((5, 40, 128), F32),
            pltpu.VMEM((5, 8, 128), F32),
            pltpu.VMEM((5, 40, 128), F32),
            pltpu.VMEM((5, 8, 128), F32),
            dma((8,)),
        ]
        + [dma((5,))] * 12,
        compiler_params=pltpu.CompilerParams(collective_id=0, has_side_effects=True, vmem_limit_bytes=48 * 2**20),
    )(positions, features, cotangent, nbr_src, nbr_tgt, pair_mask, pair_species, w_in, species_emb, w_out)


def solution(mesh):
    grid = P("gx", "gy", None, None)
    lists = P("gx", "gy", None, None, None)
    return jax.shard_map(
        local,
        mesh=mesh,
        in_specs=(grid, grid, grid, lists, lists, lists, lists, P(), P(), P()),
        out_specs=(grid, grid),
        check_vma=False,
    )
```

time: 166 us -> 49.4 us (0.30)
  the two profiles are of different devices: /device:TPU:8 before, /device:TPU:6 now
where the time goes in v1:
time: 49.4 us; the launch traced here: 48.9 us
  Pallas kernels  43.3 us (88%)
  local copies, waits for them, and re-layouts  4.93 us (10%)
  between operations  0.68 us (1%)
    pallas_call x1, Pallas kernels, local(): pl.pallas_call(kernel, out_shape=(jax.ShapeDtypeStruct(positions.shape, F...  43.3 us
    unnamed x22, local copies, waits for them, and re-layouts  4.36 us

profile of v1, /device:TPU:6, one launch (start us, length us, event | category | flops | bytes accessed | tf_op | source)
XLA Modules:
  0.0 48.9 jit_solution(11122209612919532501)
XLA Ops:
  0.6 0.7 %copy.12.pos_in = f32[1,1,3,32]{3,2,1,0:T(4,128)S(1)} copy(f32[1,1,3,32]{3,1,2,0:T(1,128)} %param.10) | data formatting | bytes 768 | tf_op args[0]
  1.3 0.0 copy-start.5
  1.3 0.0 copy-start.6
  1.3 0.7 %copy.13.src_in = s32[1,1,5,5,32]{4,3,2,1,0:T(8,128)S(1)} copy(s32[1,1,5,5,32]{4,1,3,2,0:T(1,128)} %param.13) | data formatting | bytes 6400 | tf_op args[3]
  2.0 0.0 copy-done.5
  2.1 0.0 copy-start.1
  2.1 0.0 copy-done.6
  2.1 0.0 copy-start.7
  2.1 0.7 %copy-done.7 = s32[1,1,5,5,32]{4,1,3,2,0:T(1,128)S(1)} copy-done((s32[1,1,5,5,32]{4,1,3,2,0:T(1,128)S(1)}, s32[1,1,5,5,32]{4,1,3,2,0:T(1,128)}, u32[]{:S(2)}) %copy-start.7) | copy-done | bytes 3224
  2.8 0.0 copy-start.2
  2.8 0.0 copy-start.3
  2.8 0.0 copy-start.4
  2.8 0.1 copy-done.1
  2.9 0.7 %copy-done.2 = f32[1,1,32,128]{3,2,1,0:T(8,128)S(1)} copy-done((f32[1,1,32,128]{3,2,1,0:T(8,128)S(1)}, f32[1,1,32,128]{3,2,1,0:T(8,128)}, u32[]{:S(2)}) %copy-start.2) | copy-done | bytes 16408
  3.5 0.0 copy-done.3
  3.5 0.0 copy-done.4
  3.5 0.0 copy-start
  3.5 0.9 %copy-done = f32[1,1,32,1152]{3,2,1,0:T(8,128)S(1)} copy-done((f32[1,1,32,1152]{3,2,1,0:T(8,128)S(1)}, f32[1,1,32,1152]{3,2,1,0:T(8,128)}, u32[]{:S(2)}) %copy-start) | copy-done | bytes 147480
  4.4 43.3 %shard_map.113 = (f32[1,1,3,32]{3,2,1,0:T(4,128)S(1)}, f32[1,1,32,128]{3,2,1,0:T(8,128)S(1)}) custom-call(f32[1,1,3,32]{3,2,1,0:T(4,128)S(1)} %copy.12.pos_in, f32[1,1,32,128]{3,2,1,0:T(8,128)S(1)} %copy-done.2, f32[1,1,32,1152]{3,2,1,0:T(8,128)S(1)} %copy-done, s32[1,1,5,5,32]{4,3,2,1,0:T(8,128)S(1)} %copy.13.src_in, s32[1,1,5,5,32]{4,3,2,1,0:T(8,128)S(1)} %copy.14.tgt_in, ...), custom_call_target="tpu_custom_call" | custom-call | tf_op jit(solution)/shard_map/pallas_call | solution.py:273
  47.8 0.6 %copy.17 = f32[1,1,3,32]{3,1,2,0:T(1,128)} copy(f32[1,1,3,32]{3,2,1,0:T(4,128)S(1)} %get-tuple-element.2) | data formatting | bytes 768 | tf_op jit(solution)/shard_map/pallas_call | solution.py:273
  48.3 0.6 %copy.19 = f32[1,1,32,128]{3,2,1,0:T(8,128)} copy(f32[1,1,32,128]{3,2,1,0:T(8,128)S(1)} %get-tuple-element.7) | data formatting | bytes 32768
  (3 shorter events, 0.0 us)
Async XLA Ops:
  1.3 0.7 %copy-start.5 = (s32[1,1,5,5,32]{4,1,3,2,0:T(1,128)S(1)}, s32[1,1,5,5,32]{4,1,3,2,0:T(1,128)}, u32[]{:S(2)}) copy-start(s32[1,1,5,5,32]{4,1,3,2,0:T(1,128)} %param.14) | copy-start | bytes 9604
  1.3 0.7 %copy-start.6 = (s32[1,1,5,5,32]{4,1,3,2,0:T(1,128)S(1)}, s32[1,1,5,5,32]{4,1,3,2,0:T(1,128)}, u32[]{:S(2)}) copy-start(s32[1,1,5,5,32]{4,1,3,2,0:T(1,128)} %param.15) | copy-start | bytes 9604
  2.1 0.8 %copy-start.1 = (f32[32,384]{1,0:T(8,128)S(1)}, f32[32,384]{1,0:T(8,128)}, u32[]{:S(2)}) copy-start(f32[32,384]{1,0:T(8,128)} %w_out.1) | copy-start | bytes 147460
  2.1 0.7 %copy-start.7 = (s32[1,1,5,5,32]{4,1,3,2,0:T(1,128)S(1)}, s32[1,1,5,5,32]{4,1,3,2,0:T(1,128)}, u32[]{:S(2)}) copy-start(s32[1,1,5,5,32]{4,1,3,2,0:T(1,128)} %param.16) | copy-start | bytes 9604
  2.8 0.7 %copy-start.2 = (f32[1,1,32,128]{3,2,1,0:T(8,128)S(1)}, f32[1,1,32,128]{3,2,1,0:T(8,128)}, u32[]{:S(2)}) copy-start(f32[1,1,32,128]{3,2,1,0:T(8,128)} %feat_in.1) | copy-start | bytes 49156
  2.8 0.7 %copy-start.3 = (f32[10,32]{1,0:T(8,128)S(1)}, f32[10,32]{1,0:T(8,128)}, u32[]{:S(2)}) copy-start(f32[10,32]{1,0:T(8,128)} %emb.1) | copy-start | bytes 3844
  2.8 0.7 %copy-start.4 = (f32[8,32]{1,0:T(8,128)S(1)}, f32[8,32]{1,0:T(8,128)}, u32[]{:S(2)}) copy-start(f32[8,32]{1,0:T(8,128)} %w_in.1) | copy-start | bytes 3076
  3.5 0.9 %copy-start = (f32[1,1,32,1152]{3,2,1,0:T(8,128)S(1)}, f32[1,1,32,1152]{3,2,1,0:T(8,128)}, u32[]{:S(2)}) copy-start(f32[1,1,32,1152]{3,2,1,0:T(8,128)} %cot_in.1) | copy-start | bytes 442372

commit v2 on v1

v2 whole, which is shorter than its diff:
```python
import math

import jax
import jax.numpy as jnp
from jax import lax
from jax.experimental import pallas as pl
from jax.experimental.pallas import tpu as pltpu
from jax.sharding import PartitionSpec as P

MESH = pl.DeviceIdType.MESH
SIDE = 5.0
CUTOFF = 12.0
SOFTEN = 0.25
F32 = jnp.float32
BF16 = jnp.bfloat16
NN = (((1,), (0,)), ((), ()))
NT = (((1,), (1,)), ((), ()))
AWAY = (-1, 1, -2, 2)
PARTS = 9
UNROLL = 16
COUNT = (1, 2, 2)
LANES = (256, 384, 384)
R3, R5, R15 = math.sqrt(3.0), math.sqrt(5.0), math.sqrt(15.0)


def dot(lhs, rhs, dims):
    return lax.dot_general(lhs, rhs, dims, preferred_element_type=F32)


def split2(value):
    high = value.astype(BF16).astype(F32)
    return high, value - high


def split3(value):
    high, rest = split2(value)
    middle, low = split2(rest)
    return high, middle, low


def sin_cos_pi(x):
    turns = jnp.floor(x + 0.5)
    y = (x - turns) * math.pi
    half = turns * 0.5
    sign = 1.0 - 4.0 * (half - jnp.floor(half))
    y2 = y * y
    s = -1.0 / 39916800.0 + y2 * (1.0 / 6227020800.0)
    for c in (1.0 / 362880.0, -1.0 / 5040.0, 1.0 / 120.0, -1.0 / 6.0, 1.0):
        s = s * y2 + c
    c_ = 1.0 / 479001600.0 - y2 * (1.0 / 87178291200.0)
    for c in (-1.0 / 3628800.0, 1.0 / 40320.0, -1.0 / 720.0, 1.0 / 24.0, -0.5, 1.0):
        c_ = c_ * y2 + c
    return s * y * sign, c_ * sign


def run_length(peers):
    return 12 if peers % 12 == 0 else 4


def remote(src, dst, send_sem, recv_sem, device):
    return pltpu.make_async_remote_copy(
        src_ref=src, dst_ref=dst, send_sem=send_sem, recv_sem=recv_sem, device_id=device, device_id_type=MESH
    )


def piece(ref, k):
    width = ref.shape[-1] // PARTS
    return ref.at[:, pl.ds(k * width, width)]


def kernel(
    pos_in, feat_in, cot_in, src_in, tgt_in, mask_in, spec_in, w_in_hbm, emb_hbm, w_out_hbm,
    pos_out, feat_out,
    w_in, emb, w_out, posx, posy, feats, cots, lists, wt, w_first, featt, acc, tgt_send, ret, tgt_ret, way,
    index0, index1, index2, hot0, hot1, hot2, posmat0, posmat1, posmat2, gath0, gath1, gath2,
    fbuf0, fbuf1, fbuf2, radial0, radial1, radial2, sph0, sph1, sph2, geo0, geo1, geo2, pp0, pp1, pp2,
    local_sem, fx_send, fx_recv, py_send, py_recv, px_send, px_recv, ct_send, ct_recv,
    rs_send, rs_recv, rt_send, rt_recv, w_send, w_recv, r_send, r_recv, crossed,
    st_send, st_recv, fw_send, stage_pos, m_send, m_recv, passed,
):
    index, hot, posmat = (index0, index1, index2), (hot0, hot1, hot2), (posmat0, posmat1, posmat2)
    gath, fbuf, radial = (gath0, gath1, gath2), (fbuf0, fbuf1, fbuf2), (radial0, radial1, radial2)
    sph, geo, pp = (sph0, sph1, sph2), (geo0, geo1, geo2), (pp0, pp1, pp2)
    a, b = lax.axis_index("gx"), lax.axis_index("gy")
    na, nb = lax.axis_size("gx"), lax.axis_size("gy")
    run = run_length(nb)
    place = lax.rem(b, run)
    low = place < run // 2
    far = jnp.where(low, -1, 1)

    def x_at(shift):
        return (lax.rem(a + shift + na, na), b)

    def y_at(shift):
        return (a, lax.rem(b + shift + nb, nb))

    def slots(g):
        return [2] if g == 0 else [2 - far, 2 - 2 * far] if g == 1 else [2 + far, 2 + 2 * far]

    barrier = pltpu.get_barrier_semaphore()

    def signal(semaphore, device):
        pl.semaphore_signal(semaphore, inc=1, device_id=device, device_id_type=MESH)

    for s in AWAY:
        signal(barrier, x_at(s))
    for s in (-2, -1):
        signal(barrier, y_at(s))
    for s in (1, 2):
        @pl.when(place + s < run)
        def _(s=s):
            signal(barrier, y_at(s))

    for p, shifts in ((0, (run, run - 1, run - 2)), (1, (run, run - 2, -3))):
        @pl.when(place == p)
        def _(shifts=shifts):
            for shift in shifts:
                signal(barrier, y_at(shift))

    entered = jnp.where(place == 0, 7, jnp.where(place >= run - 2, 10, 8))

    own = [
        pltpu.make_async_copy(src, dst, local_sem.at[k])
        for k, (src, dst) in enumerate(
            (
                (src_in, lists.at[0]), (tgt_in, lists.at[1]), (mask_in, lists.at[2]), (spec_in, lists.at[3]),
                (w_out_hbm, w_out), (w_in_hbm, w_in), (emb_hbm, emb), (cot_in.at[0, 0], cots.at[2]),
                (pos_in, posx.at[2]), (pos_in, posy.at[2]), (feat_in.at[0, 0], feats.at[2]),
            )
        )
    ]
    for copy in own:
        copy.start()

    def straight(k):
        return remote(piece(cot_in.at[0, 0], k), piece(cots.at[1], k), m_send.at[k], m_recv.at[k], y_at(1))

    def to_way(k):
        return remote(piece(cot_in.at[0, 0], k), piece(passed, k), w_send.at[k], w_recv.at[k], y_at(3))

    def pass_on(p, k):
        src = cots.at[1] if p == 0 else passed
        return remote(piece(src, k), piece(cots.at[0], k), r_send.at[k], r_recv.at[k], y_at(1 - 2 * p))

    def of_pos_x(s):
        return remote(pos_in, posx.at[s + 2], px_send.at[s + 2], px_recv.at[s + 2], x_at(-s))

    def of_feats(s):
        return remote(feat_in.at[0, 0], feats.at[s + 2], fx_send.at[s + 2], fx_recv.at[s + 2], x_at(-s))

    def of_pos_y(slot):
        return remote(pos_in, posy.at[slot], py_send.at[slot], py_recv.at[slot], y_at(2 - slot))

    def of_cot(slot):
        return remote(cot_in.at[0, 0], cots.at[slot], ct_send.at[slot], ct_recv.at[slot], y_at(2 - slot))

    def of_sums(s):
        return remote(acc.at[s + 2], ret.at[s + 2], rs_send.at[s + 2], rs_recv.at[s + 2], x_at(s))

    def of_targets(slot):
        return remote(tgt_send.at[slot], tgt_ret.at[slot], rt_send.at[slot], rt_recv.at[slot], y_at(slot - 2))

    def gathered_cot(g):
        pieces = [split2(cots[j]) for j in slots(g)]
        stacked = jnp.concatenate([p[0] for p in pieces] + [p[1] for p in pieces], axis=0).astype(BF16)
        target_hot = hot[g][160 : 160 + 32 * COUNT[g]]
        gath[g][...] = dot(stacked.T, jnp.concatenate([target_hot, target_hot], axis=0), NN)

    def lane_maps(g):
        lane = lax.broadcasted_iota(jnp.int32, (1, LANES[g]), 1)
        second = jnp.where(lane >= 160, 1, 0)
        return lane < 160 * COUNT[g], second, (lane - 160 * second) // 32

    def setup():
        for copy in own[:8]:
            copy.wait()
        for g in range(3):
            index[g][...] = jnp.zeros_like(index[g])
            for t, j in enumerate(slots(g)):
                for i in range(5):
                    at = 160 * t + 32 * i
                    for field in range(4):
                        index[g][field : field + 1, at : at + 32] = lists[field, 5 * i + j]
            used, second, step = lane_maps(g)
            src_row = jnp.where(used, index[g][0:1] + 32 * step, -1)
            tgt_row = jnp.where(used, index[g][1:2] + 32 * second + 160, -1)
            src_ids = lax.broadcasted_iota(jnp.int32, (160, LANES[g]), 0)
            tgt_ids = lax.broadcasted_iota(jnp.int32, (32 * COUNT[g], LANES[g]), 0) + 160
            hot[g][0:160] = (src_ids == src_row).astype(F32).astype(BF16)
            hot[g][160:] = (tgt_ids == tgt_row).astype(F32).astype(BF16)
        w_high, w_low = split2(w_out[...])
        wt[...] = jnp.concatenate([w_high, w_high, w_low], axis=0).T.astype(BF16)
        i_high, i_low = split2(w_in[...])
        e_high, e_low = split2(emb[...])
        gap = jnp.zeros((6, 32), F32)
        first = [i_high, i_high, i_low, e_high, gap, e_low, gap, jnp.zeros((8, 32), F32)]
        w_first[...] = jnp.concatenate(first, axis=0).T.astype(BF16)
        gathered_cot(0)

    pl.when(low)(setup)
    pl.semaphore_wait(barrier, entered)

    @pl.when(place == run - 1)
    def _():
        signal(crossed, y_at(1 - run))
        signal(crossed, y_at(2 - run))

    @pl.when(place == run - 2)
    def _():
        signal(crossed, y_at(2 - run))

    def whole(slot):
        kept = place + 2 - slot >= 0
        if slot == 0:
            return place < run - 2
        return place < run - 1 if slot == 1 else kept

    for slot in (0, 4, 1, 3):
        @pl.when(place + 2 - slot >= 0)
        def _(slot=slot):
            of_pos_y(slot).start()
    for s in AWAY:
        of_pos_x(s).start()
    for s in AWAY:
        of_feats(s).start()
    for p, copy in ((run - 1, straight), (run - 2, to_way)):
        @pl.when(place == p)
        def _(copy=copy):
            for k in range(PARTS):
                copy(k).start()
    for slot in (0, 4, 1, 3):
        @pl.when(whole(slot))
        def _(slot=slot):
            of_cot(slot).start()

    def stage(k):
        src, dst = ((pos_in, stage_pos), (cot_in.at[0, 0], way))[k]
        return remote(src, dst, st_send.at[k], st_recv.at[k], y_at(-run))

    def forward(k, slot, n, shift):
        src, dst = ((stage_pos, posy.at[slot]), (way, cots.at[slot]))[k]
        return remote(src, dst, fw_send.at[2 * n + k], (py_recv, ct_recv)[k].at[slot], y_at(shift))

    forwards = {0: ((3, run - 1), (4, run - 2)), 1: ((4, run - 2),)}

    @pl.when(place <= 1)
    def _():
        stage(0).start()
        stage(1).start()

    def cross():
        for p, receivers in forwards.items():
            @pl.when(place == p)
            def _(receivers=receivers):
                pl.semaphore_wait(crossed, len(receivers))
                for k in range(2):
                    stage(k).wait_recv()
                    for n, (slot, shift) in enumerate(receivers):
                        forward(k, slot, n, shift).start()

    pl.when(jnp.logical_not(low))(setup)

    def geometry(g):
        width = LANES[g]
        for t, j in enumerate(slots(g)):
            posmat[g][0:3, 160 + 32 * t : 192 + 32 * t] = -posy[j, :, 0]
        picked = dot(jnp.concatenate(split3(posmat[g][...]), axis=0).astype(BF16), hot[g][...], NN)
        picked = picked[0:8] + picked[8:16] + picked[16:24]
        used, second, step = lane_maps(g)
        rx = picked[0:1] + (step - 2).astype(F32) * SIDE
        ry, rz = picked[1:2], picked[2:3]
        if g:
            ry = ry - ((far if g == 2 else -far) * (1 + second)).astype(F32) * SIDE
        dist = jnp.sqrt(rx * rx + ry * ry + rz * rz + SOFTEN)
        inv = 1.0 / dist
        ux, uy, uz = rx * inv, ry * inv, rz * inv
        q = dist * (1.0 / CUTOFF)
        left = jnp.maximum(1.0 - q * q, 0.0)
        alive = index[g][2:3].astype(F32)
        env = left * left * alive
        denv = q * left * alive * (-4.0 / CUTOFF)
        sph[g][...] = jnp.concatenate(
            [
                R3 * ux, R3 * uy, R3 * uz,
                R15 * ux * uy, R15 * uy * uz, 0.5 * R5 * (2.0 * uz * uz - ux * ux - uy * uy),
                R15 * ux * uz, 0.5 * R15 * (ux * ux - uy * uy),
            ],
            axis=0,
        )
        geo[g][0:4] = jnp.concatenate([ux, uy, uz, inv], axis=0)
        order = (lax.broadcasted_iota(jnp.int32, (8, width), 0) + 1).astype(F32)
        root = math.sqrt(2.0 / CUTOFF)
        sine, cosine = sin_cos_pi(order * q)
        basis = root * sine * inv
        dbasis = (order * (root * math.pi / CUTOFF) * cosine - basis) * inv
        chosen = (lax.broadcasted_iota(jnp.int32, (16, width), 0) == index[g][3:4]).astype(F32)
        chosen = jnp.concatenate([chosen, jnp.zeros_like(chosen)], axis=1)
        high, rest = split2(jnp.concatenate([basis, dbasis], axis=1))
        first = jnp.concatenate([high, rest, high, chosen, chosen, jnp.zeros_like(high)], axis=0)
        both = dot(w_first[...], first.astype(BF16), NN)
        z, dz = both[:, :width], both[:, width:]
        sig = 1.0 / (1.0 + jnp.exp(-z))
        hidden = z * sig
        dhidden = sig * (1.0 + z * (1.0 - sig)) * dz
        high, rest = split2(jnp.concatenate([hidden * env, dhidden * env + hidden * denv], axis=1))
        radial[g][...] = dot(wt[...], jnp.concatenate([high, rest, high], axis=0).astype(BF16), NN)

    def main(g):
        width = LANES[g]
        columns = []
        for block in range(width // 128):
            at = 128 * block
            lanes = pl.ds(at, 128)

            def channels(c, carry, at=at, lanes=lanes):
                carry = list(carry)
                products = []
                for u in range(UNROLL):
                    r0 = pl.multiple_of(c * (8 * UNROLL) + u * 8, 8)
                    f = fbuf[g][pl.ds(r0, 8), lanes]
                    w = [gath[g][pl.ds(m * 128 + r0, 8), lanes] for m in range(9)]
                    y = [None] + [sph[g][m : m + 1, lanes] for m in range(8)]
                    rad = [radial[g][pl.ds(l * 128 + r0, 8), lanes] for l in range(3)]
                    drad = [radial[g][pl.ds(l * 128 + r0, 8), pl.ds(width + at, 128)] for l in range(3)]
                    c1 = y[1] * w[1] + y[2] * w[2] + y[3] * w[3]
                    c2 = (y[4] * w[4] + y[5] * w[5]) + (y[6] * w[6] + y[7] * w[7]) + y[8] * w[8]
                    products.append(rad[0] * w[0] + rad[1] * c1 + rad[2] * c2)
                    p1, p2 = rad[1] * f, rad[2] * f
                    carry[0] = carry[0] + f * (drad[0] * w[0] + drad[1] * c1 + drad[2] * c2)
                    for m in range(1, 9):
                        carry[m] = carry[m] + (p1 if m < 4 else p2) * w[m]
                for u in range(UNROLL):
                    pp[g][pl.ds(pl.multiple_of(c * (8 * UNROLL) + u * 8, 8), 8), lanes] = products[u]
                return tuple(carry)

            sums = lax.fori_loop(0, 16 // UNROLL, channels, tuple(jnp.zeros((8, 128), F32) for _ in range(9)))
            columns.append([jnp.sum(v, axis=0, keepdims=True) for v in sums])
        gd, *gy = [jnp.concatenate([column[m] for column in columns], axis=1) for m in range(9)]
        ux, uy, uz, inv = (geo[g][k : k + 1] for k in range(4))
        gux = R3 * gy[0] + R15 * (uy * gy[3] + uz * gy[6] + ux * gy[7]) - R5 * ux * gy[5]
        guy = R3 * gy[1] + R15 * (ux * gy[3] + uz * gy[4] - uy * gy[7]) - R5 * uy * gy[5]
        guz = R3 * gy[2] + R15 * (uy * gy[4] + ux * gy[6]) + 2.0 * R5 * uz * gy[5]
        along = gd - (gux * ux + guy * uy + guz * uz) * inv
        grad = jnp.concatenate(
            [gux * inv + along * ux, guy * inv + along * uy, guz * inv + along * uz, jnp.zeros((5, width), F32)], axis=0
        )
        scat = dot(jnp.concatenate(split2(grad), axis=0).astype(BF16), hot[g][...], NT)
        scat = scat[0:8] + scat[8:16]
        for t, j in enumerate(slots(g)):
            tgt_send[j, :, 0:32] = -scat[:, 160 + 32 * t : 192 + 32 * t]
        p_high, p_low = split2(pp[g][...])
        fscat = dot(hot[g][0:160], jnp.concatenate([p_high, p_low], axis=0).astype(BF16), NT)
        fscat = fscat[:, 0:128] + fscat[:, 128:256]
        for i in range(5):
            if g:
                acc[i, 0:32, :] += fscat[32 * i : 32 * i + 32]
                acc[i, 32:40, 0:32] += scat[:, 32 * i : 32 * i + 32]
            else:
                acc[i, 0:32, :] = fscat[32 * i : 32 * i + 32]
                acc[i, 32:40, :] = jnp.zeros((8, 128), F32)
                acc[i, 32:40, 0:32] = scat[:, 32 * i : 32 * i + 32]

    for copy in own[8:]:
        copy.wait()
    for s in AWAY:
        of_pos_x(s).wait_recv()
    for g in range(3):
        posmat[g][...] = jnp.zeros_like(posmat[g])
        for i in range(5):
            posmat[g][0:3, 32 * i : 32 * i + 32] = posx[i, :, 0]
    geometry(0)
    pl.when(low)(cross)
    for s in AWAY:
        of_feats(s).wait_recv()
    f_high, f_low = split2(jnp.concatenate([feats[i] for i in range(5)], axis=0))
    featt[...] = jnp.concatenate([f_high, f_low], axis=1).T.astype(BF16)
    for g in range(3):
        two = dot(featt[...], hot[g][0:160], NN)
        fbuf[g][...] = two[0:128] + two[128:256]
    main(0)

    for j in slots(1):
        of_pos_y(j).wait_recv()
    geometry(1)

    for j in slots(1):
        of_cot(j).wait_recv()
    gathered_cot(1)
    main(1)
    for j in slots(1):
        of_targets(j).start()

    for j in slots(2):
        of_pos_y(j).wait_recv()
    geometry(2)

    for p, copy in ((0, straight), (1, to_way)):
        @pl.when(place == p)
        def _(p=p, copy=copy):
            for k in range(PARTS):
                copy(k).wait_recv()
                pass_on(p, k).start()
            for k in range(PARTS):
                pass_on(p, k).wait_recv()

    one, two = slots(2)

    @pl.when(place != 0)
    def _():
        of_cot(one).wait_recv()

    @pl.when(place > 1)
    def _():
        of_cot(two).wait_recv()

    gathered_cot(2)
    main(2)
    for j in slots(2):
        of_targets(j).start()

    for s in AWAY:
        of_sums(s).start()
    pos_total = acc[2, 32:40, :] + tgt_send[2]
    feat_total = acc[2, 0:32, :]
    for s in AWAY:
        of_sums(s).wait_recv()
        feat_total = feat_total + ret[s + 2, 0:32, :]
        pos_total = pos_total + ret[s + 2, 32:40, :]
    feat_out[0, 0] = feat_total
    for s in AWAY:
        of_targets(s + 2).wait_recv()
        pos_total = pos_total + tgt_ret[s + 2]
    pos_out[:, 0] = pos_total[0:3, 0:32]

    for s in AWAY:
        of_pos_x(s).wait_send()
        of_feats(s).wait_send()
        of_sums(s).wait_send()
        of_targets(s + 2).wait_send()
    for slot in (0, 4, 1, 3):
        @pl.when(place + 2 - slot >= 0)
        def _(slot=slot):
            of_pos_y(slot).wait_send()

        @pl.when(whole(slot))
        def _(slot=slot):
            of_cot(slot).wait_send()
    for p, copy in ((run - 1, straight), (run - 2, to_way)):
        @pl.when(place == p)
        def _(copy=copy):
            for k in range(PARTS):
                copy(k).wait_send()
    for p in (0, 1):
        @pl.when(place == p)
        def _(p=p):
            for k in range(PARTS):
                pass_on(p, k).wait_send()

    for p, receivers in forwards.items():
        @pl.when(place == p)
        def _(receivers=receivers):
            for k in range(2):
                stage(k).wait_send()
                for n, (slot, shift) in enumerate(receivers):
                    forward(k, slot, n, shift).wait_send()


def local(positions, features, cotangent, nbr_src, nbr_tgt, pair_mask, pair_species, w_in, species_emb, w_out):
    hbm = pl.BlockSpec(memory_space=pltpu.HBM)
    vmem = pl.BlockSpec(memory_space=pltpu.VMEM)
    dma = pltpu.SemaphoreType.DMA

    def per_group(dtype, shape):
        return [pltpu.VMEM(shape(COUNT[g], LANES[g]), dtype) for g in range(3)]

    nbr = [x.transpose(0, 2, 3, 1, 4).reshape(25, 1, 32) for x in (nbr_src, nbr_tgt, pair_mask, pair_species)]
    xyz = positions.transpose(0, 2, 1, 3).reshape(3, 1, 32)
    pos_grad, feat_grad = pl.pallas_call(
        kernel,
        out_shape=(
            jax.ShapeDtypeStruct(xyz.shape, F32),
            jax.ShapeDtypeStruct(features.shape, F32),
        ),
        in_specs=[hbm] * 10,
        out_specs=(vmem, vmem),
        scratch_shapes=[
            pltpu.VMEM((8, 32), F32),
            pltpu.VMEM((10, 32), F32),
            pltpu.VMEM((32, 384), F32),
            pltpu.VMEM((5, 3, 1, 32), F32),
            pltpu.VMEM((5, 3, 1, 32), F32),
            pltpu.VMEM((5, 32, 128), F32),
            pltpu.VMEM((5, 32, 1152), F32),
            pltpu.VMEM((4, 25, 1, 32), jnp.int32),
            pltpu.VMEM((384, 96), BF16),
            pltpu.VMEM((32, 64), BF16),
            pltpu.VMEM((256, 160), BF16),
            pltpu.VMEM((5, 40, 128), F32),
            pltpu.VMEM((5, 8, 128), F32),
            pltpu.VMEM((5, 40, 128), F32),
            pltpu.VMEM((5, 8, 128), F32),
            pltpu.VMEM((32, 1152), F32),
            *per_group(jnp.int32, lambda n, w: (4, w)),
            *per_group(BF16, lambda n, w: (160 + 32 * n, w)),
            *per_group(F32, lambda n, w: (8, 160 + 32 * n)),
            *per_group(F32, lambda n, w: (1152, w)),
            *per_group(F32, lambda n, w: (128, w)),
            *per_group(F32, lambda n, w: (384, 2 * w)),
            *per_group(F32, lambda n, w: (8, w)),
            *per_group(F32, lambda n, w: (8, w)),
            *per_group(F32, lambda n, w: (128, w)),
            dma((11,)),
            *[dma((5,))] * 12,
            *[dma((PARTS,))] * 4,
            pltpu.SemaphoreType.REGULAR,
            dma((2,)),
            dma((2,)),
            dma((4,)),
            pltpu.VMEM((3, 1, 32), F32),
            dma((PARTS,)),
            dma((PARTS,)),
            pltpu.VMEM((32, 1152), F32),
        ],
        compiler_params=pltpu.CompilerParams(collective_id=0, has_side_effects=True, vmem_limit_bytes=56 * 2**20),
    )(xyz, features, cotangent, *nbr, w_in, species_emb, w_out)
    return pos_grad.reshape(1, 3, 1, 32).transpose(0, 2, 1, 3), feat_grad


def solution(mesh):
    grid = P("gx", "gy", None, None)
    lists = P("gx", "gy", None, None, None)
    return jax.shard_map(
        local,
        mesh=mesh,
        in_specs=(grid, grid, grid, lists, lists, lists, lists, P(), P(), P()),
        out_specs=(grid, grid),
        check_vma=False,
    )
```

time: 49.4 us -> 41.6 us (0.84)
  the two profiles are of different devices: /device:TPU:6 before, /device:TPU:8 now
where the time goes in v2:
time: 41.6 us; the launch traced here: 41.3 us
  Pallas kernels  38.1 us (92%)
  local copies, waits for them, and re-layouts  2.54 us (6%)
  between operations  0.65 us (2%)
    pallas_call x1, Pallas kernels, local(): pl.pallas_call(kernel, out_shape=(jax.ShapeDtypeStruct(xyz.shape, F32), j...  38.1 us
    unnamed x4, local copies, waits for them, and re-layouts  2.54 us

profile of v2, /device:TPU:8, one launch (start us, length us, event | category | flops | bytes accessed | tf_op | source)
XLA Modules:
  0.0 41.3 jit_solution(9642297006599188816)
XLA Ops:
  0.6 38.1 %shard_map.113 = (f32[3,1,32]{2,1,0:T(1,128)}, f32[1,1,32,128]{3,2,1,0:T(8,128)}) custom-call(f32[3,1,32]{2,1,0:T(1,128)} %bitcast.12, f32[1,1,32,128]{3,2,1,0:T(8,128)} %feat_in.1, f32[1,1,32,1152]{3,2,1,0:T(8,128)} %cot_in.1, s32[25,1,32]{2,1,0:T(1,128)} %bitcast.8, s32[25,1,32]{2,1,0:T(1,128)} %bitcast.9, s32[25,1,32]{2,1,0:T(1,128)} %bitcast.10, ...), custom_call_target="tpu_custom_call" | custom-call | tf_op jit(solution)/shard_map/pallas_call | solution.py:478
  38.7 0.0 copy-start
  38.7 0.7 %copy-done = f32[3,1,32]{2,1,0:T(1,128)S(1)} copy-done((f32[3,1,32]{2,1,0:T(1,128)S(1)}, f32[3,1,32]{2,1,0:T(1,128)}, u32[]{:S(2)}) %copy-start) | copy-done | bytes 408
  39.4 0.6 %copy.15 = f32[1,1,3,32]{3,1,2,0:T(1,128)} copy(f32[1,1,3,32]{3,1,2,0:T(1,128)S(1)} %bitcast.13) | data formatting | bytes 768
  39.9 1.3 %copy.16 = f32[1,1,32,128]{3,2,1,0:T(8,128)} copy(f32[1,1,32,128]{3,2,1,0:T(8,128)} %get-tuple-element.11) | data formatting | bytes 32768
Async XLA Ops:
  38.7 0.7 %copy-start = (f32[3,1,32]{2,1,0:T(1,128)S(1)}, f32[3,1,32]{2,1,0:T(1,128)}, u32[]{:S(2)}) copy-start(f32[3,1,32]{2,1,0:T(1,128)} %get-tuple-element.4) | copy-start | bytes 1156

commit v3 on v2

--- a/solution.py
+++ b/solution.py
@@ -16,7 +16,7 @@
 NN = (((1,), (0,)), ((), ()))
 NT = (((1,), (1,)), ((), ()))
 AWAY = (-1, 1, -2, 2)
-PARTS = 9
+PARTS = 3
 UNROLL = 16
 COUNT = (1, 2, 2)
 LANES = (256, 384, 384)
@@ -70,7 +70,7 @@
 
 def kernel(
     pos_in, feat_in, cot_in, src_in, tgt_in, mask_in, spec_in, w_in_hbm, emb_hbm, w_out_hbm,
-    pos_out, feat_out,
+    sums_out,
     w_in, emb, w_out, posx, posy, feats, cots, lists, wt, w_first, featt, acc, tgt_send, ret, tgt_ret, way,
     index0, index1, index2, hot0, hot1, hot2, posmat0, posmat1, posmat2, gath0, gath1, gath2,
     fbuf0, fbuf1, fbuf2, radial0, radial1, radial2, sph0, sph1, sph2, geo0, geo1, geo2, pp0, pp1, pp2,
@@ -137,6 +137,10 @@
 
     def to_way(k):
         return remote(piece(cot_in.at[0, 0], k), piece(passed, k), w_send.at[k], w_recv.at[k], y_at(3))
+
+    def last():
+        k = PARTS - 1
+        return remote(piece(cot_in.at[0, 0], k), piece(cots.at[0], k), r_send.at[k], r_recv.at[k], y_at(2))
 
     def pass_on(p, k):
         src = cots.at[1] if p == 0 else passed
@@ -223,12 +227,20 @@
         of_pos_x(s).start()
     for s in AWAY:
         of_feats(s).start()
-    for p, copy in ((run - 1, straight), (run - 2, to_way)):
-        @pl.when(place == p)
-        def _(copy=copy):
-            for k in range(PARTS):
-                copy(k).start()
-    for slot in (0, 4, 1, 3):
+    @pl.when(place == run - 1)
+    def _():
+        for k in range(PARTS - 1):
+            straight(k).start()
+        last().start()
+        straight(PARTS - 1).start()
+
+    @pl.when(place == run - 2)
+    def _():
+        for k in range(PARTS - 1):
+            to_way(k).start()
+        last().start()
+
+    for slot in (1, 3, 0, 4):
         @pl.when(whole(slot))
         def _(slot=slot):
             of_cot(slot).start()
@@ -397,11 +409,14 @@
     for p, copy in ((0, straight), (1, to_way)):
         @pl.when(place == p)
         def _(p=p, copy=copy):
-            for k in range(PARTS):
+            for k in range(PARTS - 1):
                 copy(k).wait_recv()
                 pass_on(p, k).start()
-            for k in range(PARTS):
+            if p == 0:
+                straight(PARTS - 1).wait_recv()
+            for k in range(PARTS - 1):
                 pass_on(p, k).wait_recv()
+            last().wait_recv()
 
     one, two = slots(2)
 
@@ -426,11 +441,11 @@
         of_sums(s).wait_recv()
         feat_total = feat_total + ret[s + 2, 0:32, :]
         pos_total = pos_total + ret[s + 2, 32:40, :]
-    feat_out[0, 0] = feat_total
+    sums_out[0:32] = feat_total
     for s in AWAY:
         of_targets(s + 2).wait_recv()
         pos_total = pos_total + tgt_ret[s + 2]
-    pos_out[:, 0] = pos_total[0:3, 0:32]
+    sums_out[32:40] = pos_total
 
     for s in AWAY:
         of_pos_x(s).wait_send()
@@ -445,15 +460,16 @@
         @pl.when(whole(slot))
         def _(slot=slot):
             of_cot(slot).wait_send()
-    for p, copy in ((run - 1, straight), (run - 2, to_way)):
+    for p, copy, count in ((run - 1, straight, PARTS), (run - 2, to_way, PARTS - 1)):
         @pl.when(place == p)
-        def _(copy=copy):
-            for k in range(PARTS):
+        def _(copy=copy, count=count):
+            for k in range(count):
                 copy(k).wait_send()
+            last().wait_send()
     for p in (0, 1):
         @pl.when(place == p)
         def _(p=p):
-            for k in range(PARTS):
+            for k in range(PARTS - 1):
                 pass_on(p, k).wait_send()
 
     for p, receivers in forwards.items():
@@ -465,6 +481,11 @@
                     forward(k, slot, n, shift).wait_send()
 
 
+def split(sums, pos_out, feat_out):
+    feat_out[0, 0] = sums[0:32]
+    pos_out[:, 0] = sums[32:35, 0:32]
+
+
 def local(positions, features, cotangent, nbr_src, nbr_tgt, pair_mask, pair_species, w_in, species_emb, w_out):
     hbm = pl.BlockSpec(memory_space=pltpu.HBM)
     vmem = pl.BlockSpec(memory_space=pltpu.VMEM)
@@ -475,14 +496,11 @@
 
     nbr = [x.transpose(0, 2, 3, 1, 4).reshape(25, 1, 32) for x in (nbr_src, nbr_tgt, pair_mask, pair_species)]
     xyz = positions.transpose(0, 2, 1, 3).reshape(3, 1, 32)
-    pos_grad, feat_grad = pl.pallas_call(
+    sums = pl.pallas_call(
         kernel,
-        out_shape=(
-            jax.ShapeDtypeStruct(xyz.shape, F32),
-            jax.ShapeDtypeStruct(features.shape, F32),
-        ),
+        out_shape=jax.ShapeDtypeStruct((40, 128), F32),
         in_specs=[hbm] * 10,
-        out_specs=(vmem, vmem),
+        out_specs=vmem,
         scratch_shapes=[
             pltpu.VMEM((8, 32), F32),
             pltpu.VMEM((10, 32), F32),
@@ -523,6 +541,12 @@
         ],
         compiler_params=pltpu.CompilerParams(collective_id=0, has_side_effects=True, vmem_limit_bytes=56 * 2**20),
     )(xyz, features, cotangent, *nbr, w_in, species_emb, w_out)
+    pos_grad, feat_grad = pl.pallas_call(
+        split,
+        out_shape=(jax.ShapeDtypeStruct(xyz.shape, F32), jax.ShapeDtypeStruct(features.shape, F32)),
+        in_specs=[vmem],
+        out_specs=(vmem, vmem),
+    )(sums)
     return pos_grad.reshape(1, 3, 1, 32).transpose(0, 2, 1, 3), feat_grad
 
 

time: 41.6 us -> 39.9 us (0.959)
  local copies, waits for them, and re-layouts: 2.54 us -> 0 us
  Pallas kernels: 38.1 us -> 39.1 us
    unnamed x4 -> x0, local copies, waits for them, and re-layouts: 2.54 us -> none
    pallas_call x1 -> x2, Pallas kernels: 38.1 us -> 39.1 us  [the longest x1 37.7 us: local(): pl.pallas_call(kernel, out_shape=jax.ShapeDtypeStruct((40, 128), F32), in...]
where the time goes in v3:
time: 39.9 us; the launch traced here: 39.7 us
  Pallas kernels  39.1 us (98%)
  between operations  0.64 us (2%)
    pallas_call x1, Pallas kernels, local(): pl.pallas_call(kernel, out_shape=jax.ShapeDtypeStruct((40, 128), F32), in...  37.7 us
    pallas_call x1, Pallas kernels, local(): pl.pallas_call(split, out_shape=(jax.ShapeDtypeStruct(xyz.shape, F32), ja...  1.34 us

profile of v3, /device:TPU:8, one launch (start us, length us, event | category | flops | bytes accessed | tf_op | source)
XLA Modules:
  0.0 39.7 jit_solution(16566537502709281527)
XLA Ops:
  0.6 37.7 %shard_map.113.sums = f32[40,128]{1,0:T(8,128)} custom-call(f32[3,1,32]{2,1,0:T(1,128)} %bitcast.12, f32[1,1,32,128]{3,2,1,0:T(8,128)} %feat_in.1, f32[1,1,32,1152]{3,2,1,0:T(8,128)} %cot_in.1, s32[25,1,32]{2,1,0:T(1,128)} %bitcast.8, s32[25,1,32]{2,1,0:T(1,128)} %bitcast.9, s32[25,1,32]{2,1,0:T(1,128)} %bitcast.10, s32[25,1,32]{2,1,0:T(1,128)} %bitcast.11, ...), custom_call_target="tpu_custom_call" | custom-call | tf_op jit(solution)/shard_map/pallas_call | solution.py:499
  38.4 1.3 %shard_map.114 = (f32[3,1,32]{2,1,0:T(1,128)}, f32[1,1,32,128]{3,2,1,0:T(8,128)}) custom-call(f32[40,128]{1,0:T(8,128)} %shard_map.113.sums), custom_call_target="tpu_custom_call" | custom-call | tf_op jit(solution)/shard_map/pallas_call | solution.py:544
